TPU v7x, 512 devices: a whole 4x4x16 slice. The times are simulated.
512 devices in a mesh: clusters: 32 (over z, core), group: 16 (over x, y).
Axes of the slice: x: 4, y: 4, z: 16, core: 2. Of those that a mesh axis runs over, the one named last changes fastest.
Arguments:
- embeddings: bfloat16 [262144, 1024], P(('clusters', 'group')), may hold values from -20 to 20
- new_label: int32 [262144], P(('clusters', 'group')), may hold values from 0 to 31, as said below
- dest_member: int32 [262144], P(('clusters', 'group')), may hold values from 0 to 15, as said below
- seed_index: int32 [32, 512], P('clusters'), may hold values from 0 to 8191, as said below
- kappa: float32 [32], P('clusters'), may hold values from 8 to 400
Outputs:
- centroids: bfloat16 [16384, 1024], P('clusters')
- row_score: float32 [524288], P(('clusters', 'group'))
Inputs may be any that keep to these rules, and one draw needn't show every extreme that they name: `new_label`: each device sends between 192 and 320 of its rows to devices of other coarse clusters, at most 1 to any one device; in every draw one device receives exactly 1 row from every device of the other clusters, and every device sends exactly 1 row to some device. Rows whose label is their own device's cluster stay. `dest_member`: A row whose new_label is its own device's cluster has its own device's index along group here. `seed_index`: the 512 entries of cluster c are distinct positions m * 512 + s among the rows held before the move by cluster c's devices (m along group, s the row on that device), each naming a row whose new_label is c.
All inputs are finite; a program needn't handle non-finite values.
Results may differ from a plain program's by a relative error of at most 0.02.
The roundings to bfloat16 on the way count: a program that leaves them out, or rounds other values in their place, can miss the bound.
Values may be sent and summed in bfloat16 or wider, within the bound.
A program may use at most 64 MiB of HBM per device.

v0:
```python
import jax
import jax.numpy as jnp
from jax import lax
from jax.sharding import PartitionSpec as P

ITERS = 2


EPSILON = 1e-06


def unit_rows(embedded):
    values = embedded.astype(jnp.float32)
    scale = lax.rsqrt(jnp.sum(values * values, axis=-1, keepdims=True) + EPSILON)
    return (values * scale).astype(jnp.bfloat16)


def expectation(normed, alive, centres, concentration):
    scores = concentration * jnp.einsum(
        "sd,kd->sk", normed, centres, preferred_element_type=jnp.float32
    )
    largest = jnp.max(scores, axis=-1, keepdims=True)
    powered = jnp.exp(scores - largest)
    summed = jnp.sum(powered, axis=-1, keepdims=True)
    weights = (powered / summed * alive[:, None]).astype(jnp.bfloat16)
    log_norm = (largest[:, 0] + jnp.log(summed[:, 0])) * alive
    return (weights, log_norm)


def normalise(summed):
    length = jnp.sqrt(jnp.sum(summed * summed, axis=-1, keepdims=True))
    return (summed / jnp.maximum(length, 1.0)).astype(jnp.bfloat16)


def outgoing_rows(normed, moving, target, capacity, device_count):
    row_count = normed.shape[0]
    positions = jnp.arange(row_count, dtype=jnp.int32)
    matches = (
        (target[:, None] == target[None, :])
        & (positions[None, :] < positions[:, None])
        & moving[None, :]
    )
    earlier = jnp.sum(matches, axis=1)
    slot_index = jnp.where(moving, target * capacity + earlier, device_count * capacity)
    source_row = (
        jnp.full((device_count * capacity,), row_count, jnp.int32)
        .at[slot_index]
        .set(positions, mode="drop")
    )
    padded = jnp.concatenate([normed, jnp.zeros((1, normed.shape[1]), jnp.bfloat16)], axis=0)
    return (padded[source_row], (source_row < row_count).astype(jnp.bfloat16))


def shards(embeddings, new_label, dest_member, seed_index, kappa):
    row_count, feature_width = embeddings.shape
    cluster_count = lax.axis_size("clusters")
    member_count = lax.axis_size("group")
    device_count = cluster_count * member_count
    own_cluster = lax.axis_index("clusters")
    own_member = lax.axis_index("group")
    movers_most = row_count * 5 // 8
    other_devices = (cluster_count - 1) * member_count
    capacity = (movers_most + other_devices - 1) // other_devices
    normed = unit_rows(embeddings)
    moving = new_label != own_cluster
    target = new_label * member_count + dest_member
    leaving, filled = outgoing_rows(normed, moving, target, capacity, device_count)
    leaving = leaving.reshape(cluster_count, member_count, capacity, feature_width)
    filled = filled.reshape(cluster_count, member_count, capacity)
    arrived, occupied = (
        lax.all_to_all(
            lax.all_to_all(leaving, "clusters", split_axis=0, concat_axis=0, tiled=True),
            "group",
            split_axis=1,
            concat_axis=1,
            tiled=True,
        ),
        lax.all_to_all(
            lax.all_to_all(filled, "clusters", split_axis=0, concat_axis=0, tiled=True),
            "group",
            split_axis=1,
            concat_axis=1,
            tiled=True,
        ),
    )
    seed_rows = seed_index.reshape(-1)
    local_pos = seed_rows - own_member * row_count
    held_here = (local_pos >= 0) & (local_pos < row_count)
    chosen = jnp.where(
        held_here[:, None],
        normed[jnp.clip(local_pos, 0, row_count - 1)],
        jnp.zeros((), jnp.bfloat16),
    )
    centres = lax.psum(chosen.astype(jnp.float32).astype(jnp.bfloat16), "group")
    concentration = kappa[0]
    incoming = arrived.reshape(-1, feature_width)
    alive_in = occupied.reshape(-1).astype(jnp.float32)
    alive_own = jnp.where(moving, 0.0, 1.0).astype(jnp.float32)
    norm_own = alive_own
    norm_in = alive_in
    for iteration in range(ITERS):
        weights_own, norm_own = expectation(normed, alive_own, centres, concentration)
        weights_in, norm_in = expectation(incoming, alive_in, centres, concentration)
        partial_value = jnp.einsum(
            "sk,sd->kd", weights_own, normed, preferred_element_type=jnp.float32
        )
        partial_value = partial_value + jnp.einsum(
            "sk,sd->kd", weights_in, incoming, preferred_element_type=jnp.float32
        )
        centres = normalise(
            lax.psum(partial_value.astype(jnp.bfloat16), "group").astype(jnp.float32)
        )
    return (centres, jnp.concatenate([norm_own, norm_in]))


def solution(mesh):
    return jax.shard_map(
        shards,
        mesh=mesh,
        in_specs=(
            P(("clusters", "group"), None),
            P(("clusters", "group")),
            P(("clusters", "group")),
            P("clusters", None),
            P("clusters"),
        ),
        out_specs=(P("clusters", None), P(("clusters", "group"))),
        check_vma=False,
    )
```

profile of v0, /device:TPU:1, one launch (start us, length us, event | category | flops | bytes accessed | tf_op | source)
XLA Modules:
  0.0 431.2 jit_solution(14022457909516345308)
XLA Ops:
  8.8 2.4 scatter_custom_fusion
  12.0 16.7 %all-to-all-start.2 = ((bf16[32,16,1]{1,2,0:T(2,128)(2,1)}), bf16[32,16,1]{1,2,0:T(2,128)(2,1)S(1)}, u32[]{:S(2)}, u32[]{:S(2)}) async-start(bf16[32,16,1]{1,2,0:T(2,128)(2,1)} %reshape.128), calls=%async_computation.2 | async-start | bytes 32768 | tf_op jit(solution)/shard_map/all_to_all | solution.py:79
  28.8 1.5 fusion
  30.3 1.5 fusion.1
  31.8 2.8 gather_fusion.1
  34.6 5.9 %all-to-all-done.2 = bf16[32,16,1]{1,2,0:T(2,128)(2,1)S(1)} async-done(((bf16[32,16,1]{1,2,0:T(2,128)(2,1)}), bf16[32,16,1]{1,2,0:T(2,128)(2,1)S(1)}, u32[]{:S(2)}, u32[]{:S(2)}) %all-to-all-start.2) | async-done | bytes 1056 | tf_op jit(solution)/shard_map/all_to_all | solution.py:79
  40.5 6.5 %all-to-all-start = ((bf16[32,16,1,1024]{3,1,2,0:T(8,128)(2,1)}), bf16[32,16,1,1024]{3,1,2,0:T(8,128)(2,1)S(1)}, u32[]{:S(2)}, u32[]{:S(2)}) async-start(bf16[32,16,1,1024]{3,1,2,0:T(8,128)(2,1)} %bitcast.4), calls=%async_computation | async-start | bytes 2097152 | tf_op jit(solution)/shard_map/all_to_all | solution.py:72
  47.0 2.1 gather_fusion
  51.0 51.7 %all-to-all-done = bf16[32,16,1,1024]{3,1,2,0:T(8,128)(2,1)S(1)} async-done(((bf16[32,16,1,1024]{3,1,2,0:T(8,128)(2,1)}), bf16[32,16,1,1024]{3,1,2,0:T(8,128)(2,1)S(1)}, u32[]{:S(2)}, u32[]{:S(2)}) %all-to-all-start) | async-done | bytes 1048608 | tf_op jit(solution)/shard_map/all_to_all | solution.py:72
  102.7 6.8 %all-to-all-start.3 = ((bf16[32,16,1]{0,2,1:T(2,128)(2,1)}), bf16[32,16,1]{0,2,1:T(2,128)(2,1)S(1)}, u32[]{:S(2)}, u32[]{:S(2)}) async-start(bf16[32,16,1]{0,2,1:T(2,128)(2,1)} %copy.28), calls=%async_computation.3 | async-start | bytes 16384 | tf_op jit(solution)/shard_map/all_to_all | solution.py:78
  110.1 1.6 copy.25
  111.6 4.2 all-to-all-done.3
  115.9 3.7 all-to-all-start.1
  119.7 49.2 %all-reduce.5.cloned.1.call-done = bf16[512,1024]{1,0:T(8,128)(2,1)} async-done(((bf16[512,1024]{1,0:T(8,128)(2,1)}), bf16[512,1024]{1,0:T(8,128)(2,1)}) %all-reduce.5.cloned.1.call-update) | async-done | bytes 1048592 | tf_op jit(solution)/shard_map/psum | solution.py:94
  169.0 2.0 fusion.30
  171.1 2.1 fusion.12
  176.0 1.7 add_convert_fusion.1
  178.0 117.4 %all-reduce.7.cloned.1.call-done = bf16[512,1024]{1,0:T(8,128)(2,1)} async-done(((bf16[512,1024]{1,0:T(8,128)(2,1)}), bf16[512,1024]{1,0:T(8,128)(2,1)}) %all-reduce.7.cloned.1.call-update) | async-done | bytes 1048592 | tf_op jit(solution)/shard_map/psum | solution.py:111
  295.4 1.5 fusion.2
  296.9 2.0 fusion.32
  301.3 1.7 add_convert_fusion
  303.6 117.0 %all-reduce.9.cloned.1.call-done = bf16[512,1024]{1,0:T(8,128)(2,1)} async-done(((bf16[512,1024]{1,0:T(8,128)(2,1)}), bf16[512,1024]{1,0:T(8,128)(2,1)}) %all-reduce.9.cloned.1.call-update) | async-done | bytes 1048592 | tf_op jit(solution)/shard_map/psum | solution.py:111
  420.6 1.5 fusion.4
  422.2 2.5 fusion.5
  (46 shorter events, 10.8 us)
Async XLA Ops:
  12.0 28.5 %all-to-all-start.2 = ((bf16[32,16,1]{1,2,0:T(2,128)(2,1)}), bf16[32,16,1]{1,2,0:T(2,128)(2,1)S(1)}, u32[]{:S(2)}, u32[]{:S(2)}) async-start(bf16[32,16,1]{1,2,0:T(2,128)(2,1)} %reshape.128), calls=%async_computation.2 | async-start | bytes 32768 | tf_op jit(solution)/shard_map/all_to_all | solution.py:79
  34.6 12.4 %copy-start.1 = (s32[1,512]{1,0:T(1,128)S(1)}, s32[1,512]{1,0:T(1,128)}, u32[]{:S(2)}) copy-start(s32[1,512]{1,0:T(1,128)} %param.8) | copy-start | bytes 6148
  40.5 62.2 %all-to-all-start = ((bf16[32,16,1,1024]{3,1,2,0:T(8,128)(2,1)}), bf16[32,16,1,1024]{3,1,2,0:T(8,128)(2,1)S(1)}, u32[]{:S(2)}, u32[]{:S(2)}) async-start(bf16[32,16,1,1024]{3,1,2,0:T(8,128)(2,1)} %bitcast.4), calls=%async_computation | async-start | bytes 2097152 | tf_op jit(solution)/shard_map/all_to_all | solution.py:72
  47.0 122.0 %all-reduce.5.cloned.1.call-start = ((), (), s32[]{:S(2)}) async-start(), calls=%async_computation.4 | async-start | bytes 2097152 | tf_op jit(solution)/shard_map/psum | solution.py:94
  102.7 13.2 %all-to-all-start.3 = ((bf16[32,16,1]{0,2,1:T(2,128)(2,1)}), bf16[32,16,1]{0,2,1:T(2,128)(2,1)S(1)}, u32[]{:S(2)}, u32[]{:S(2)}) async-start(bf16[32,16,1]{0,2,1:T(2,128)(2,1)} %copy.28), calls=%async_computation.3 | async-start | bytes 16384 | tf_op jit(solution)/shard_map/all_to_all | solution.py:78
  115.9 57.4 %all-to-all-start.1 = ((bf16[32,16,1,1024]{3,0,2,1:T(8,128)(2,1)}), bf16[32,16,1,1024]{3,0,2,1:T(8,128)(2,1)S(1)}, u32[]{:S(2)}, u32[]{:S(2)}) async-start(bf16[32,16,1,1024]{3,0,2,1:T(8,128)(2,1)} %copy.25), calls=%async_computation.1 | async-start | bytes 2097152 | tf_op jit(solution)/shard_map/all_to_all | solution.py:71
  119.5 175.8 %all-reduce.7.cloned.1.call-start = ((), (), s32[]{:S(2)}) async-start(), calls=%async_computation.5 | async-start | bytes 2097152 | tf_op jit(solution)/shard_map/psum | solution.py:111
  173.2 1.2 copy-start.2
  174.4 1.6 copy-start.3
  177.8 242.9 %all-reduce.9.cloned.1.call-start = ((), (), s32[]{:S(2)}) async-start(), calls=%async_computation.6 | async-start | bytes 2097152 | tf_op jit(solution)/shard_map/psum | solution.py:111
  299.1 1.2 copy-start
Sparse Core Ops, SparseCore 0:
  51.6 117.3 all-reduce.4
  177.9 117.4 all-reduce.6
  303.1 117.4 all-reduce.8
where the time goes:
time: 432 us; the launch traced here: 431 us
  waiting for transfers between devices  345 us (80%)
  starting transfers between devices  33.9 us (8%)
  between operations  14.6 us (3%)
  other arithmetic  12.8 us (3%)
  local copies, waits for them, and re-layouts  12.8 us (3%)
  matrix products  11.7 us (3%)
    psum x2, waiting for transfers between devices, shards(): lax.psum(partial_value.astype(jnp.bfloat16), 'group').astype(jnp.float32)  234 us
    all_to_all x1, waiting for transfers between devices, shards(): lax.all_to_all(leaving, 'clusters', split_axis=0, concat_axis=0, tiled=True)  51.7 us
    psum x1, waiting for transfers between devices, shards(): centres = lax.psum(chosen.astype(jnp.float32).astype(jnp.bfloat16), 'group')  49.2 us
    all_to_all x1, starting transfers between devices, shards(): lax.all_to_all(filled, 'clusters', split_axis=0, concat_axis=0, tiled=True)  16.7 us
  transfers between devices with their start and end apart: 7, of which 6 were waited for; matrix products, arithmetic and copies ran while one was open for 4% of the time, Pallas kernels for 0%

commit v1 on v0

v1 whole, which is shorter than its diff:
```python
import functools

import jax
import jax.numpy as jnp
from jax import lax
from jax.experimental import pallas as pl
from jax.experimental.pallas import tpu as pltpu
from jax.sharding import PartitionSpec as P

ITERS = 2
EPSILON = 1e-06
MESH = pl.DeviceIdType.MESH
F32 = jnp.float32
BF16 = jnp.bfloat16
I32 = jnp.int32


def iota(shape, dim):
    return lax.broadcasted_iota(I32, shape, dim)


def onehot(cond):
    return jnp.where(cond, 1.0, 0.0).astype(BF16)


def nn(a, b):
    return lax.dot_general(a, b, (((1,), (0,)), ((), ())), preferred_element_type=F32)


def nt(a, b):
    return lax.dot_general(a, b, (((1,), (1,)), ((), ())), preferred_element_type=F32)


def tn(a, b):
    return lax.dot_general(a, b, (((0,), (0,)), ((), ())), preferred_element_type=F32)


def rows_at(index, size):
    return pl.ds(pl.multiple_of(index * size, size), size)


def split3(v):
    hi = v.astype(BF16)
    rest = v - hi.astype(F32)
    mid = rest.astype(BF16)
    low = (rest - mid.astype(F32)).astype(BF16)
    pad = jnp.zeros((13,) + v.shape[1:], F32)
    return jnp.concatenate([hi.astype(F32), mid.astype(F32), low.astype(F32), pad], axis=0).astype(BF16)


def kernel(
    dims,
    x_ref, label_ref, member_ref, seed_ref, kappa_ref,
    cent_ref, score_ref,
    rows, hot, send_a, send_b, mid_a, mid_b, fwd_a, fwd_b,
    weights, part, gather_in, block_out, centres, alive, norms,
    mark_s, mark_1, mark_2, mark_3, flat,
    send_sem, recv_sem,
):
    C, G, R, D, K = dims
    Z = C // 2
    S = Z * G
    kb = K // G
    c = lax.axis_index("clusters")
    g = lax.axis_index("group")
    z = c // 2
    core = lax.rem(c, 2)

    barrier = pltpu.get_barrier_semaphore()
    for i in range(1, C):
        pl.semaphore_signal(barrier, inc=1, device_id=(lax.rem(c + i, C), g), device_id_type=MESH)
    for i in range(1, G):
        pl.semaphore_signal(barrier, inc=1, device_id=(c, lax.rem(g + i, G)), device_id_type=MESH)

    def send(phase, src, dst, device):
        pltpu.make_async_remote_copy(
            src_ref=src, dst_ref=dst, send_sem=send_sem.at[phase], recv_sem=recv_sem.at[phase],
            device_id=device, device_id_type=MESH,
        ).start()

    def wait_recv(phase, ref):
        pltpu.make_async_copy(ref, ref, recv_sem.at[phase]).wait()

    def wait_send(phase, ref):
        pltpu.make_async_copy(ref, ref, send_sem.at[phase]).wait()

    ncol = min(D, 256)

    def product(dst, dst_rows, lhs, rhs_ref, rhs_rows):
        @pl.loop(0, D // ncol)
        def _(j):
            cols = rows_at(j, ncol)
            dst[dst_rows, cols] = nn(lhs, rhs_ref[rhs_rows, cols]).astype(BF16)

    rstep = min(R, 128)

    @pl.loop(0, R // rstep)
    def _(i):
        at = rows_at(i, rstep)
        v = x_ref[at, :].astype(F32)
        scale = lax.rsqrt(jnp.sum(v * v, axis=-1, keepdims=True) + EPSILON)
        rows[at, :] = (v * scale).astype(BF16)

    label = label_ref[...]
    member = member_ref[...]
    moving = label != c
    lz = lax.shift_right_logical(label, 1)
    same = (label & 1) == core
    to_a = jnp.where(moving & same, lz * G + member, -1)
    to_b = jnp.where(moving & jnp.logical_not(same), member * Z + lz, -1)
    own = pl.ds(0, R)

    hot[0:S, 0:R] = onehot(iota((S, R), 0) == to_a)
    product(send_a, slice(None), hot[0:S, 0:R], rows, own)
    pl.semaphore_wait(barrier, C - 1 + G - 1)
    for i in range(1, Z):
        tz = lax.rem(z + i, Z)
        send(0, send_a.at[rows_at(tz, G)], mid_a.at[rows_at(z, G)], (tz * 2 + core, g))
    hot[0:S, 0:R] = onehot(iota((S, R), 0) == to_b)
    product(send_b, slice(None), hot[0:S, 0:R], rows, own)
    for i in range(1, G):
        tg = lax.rem(g + i, G)
        send(1, send_b.at[rows_at(tg, Z)], mid_b.at[rows_at(g, Z)], (c, tg))
    mid_a[rows_at(z, G), :] = send_a[rows_at(z, G), :]
    mid_b[rows_at(g, Z), :] = send_b[rows_at(g, Z), :]

    to_cluster = onehot((iota((128, R), 0) == label) & moving)
    to_member = onehot(iota((128, R), 0) == member)
    marks = nt(to_cluster, to_member)
    for i in range(C):
        mark_s[i] = marks[i:i + 1, :]
    for i in range(1, C):
        tc = lax.rem(c + i, C)
        send(2, mark_s.at[tc], mark_1.at[c], (tc, g))
    mark_1[c] = mark_s[c]

    hot[0:R, 0:K] = onehot(iota((R, K), 0) + g * R == seed_ref[...])

    @pl.loop(0, D // ncol)
    def _(j):
        cols = rows_at(j, ncol)
        part[:, cols] = tn(hot[0:R, 0:K], rows[own, cols]).astype(BF16)

    def scatter(phase, first, last):
        for b in range(first, last):
            @pl.when(b != g)
            def _():
                send(phase, part.at[pl.ds(b * kb, kb)], gather_in.at[g], (c, b))

    def gathered_sum(phase):
        wait_recv(phase, gather_in.at[pl.ds(0, G - 1)])
        gather_in[g] = part[rows_at(g, kb), :]
        return jnp.sum(gather_in[...].astype(F32), axis=0)

    def spread(phase, block):
        block_out[...] = block
        for i in range(1, G):
            send(phase, block_out, centres.at[rows_at(g, kb)], (c, lax.rem(g + i, G)))
        centres[rows_at(g, kb), :] = block

    def spread_wait(phase):
        wait_recv(phase, centres.at[pl.ds(0, (G - 1) * kb)])

    scatter(3, 0, G)

    turn_b = onehot((iota((S, S), 0) & (G - 1)) * Z + lax.div(iota((S, S), 0), G) == iota((S, S), 1))
    wait_recv(1, mid_b.at[pl.ds(0, S - Z)])
    product(fwd_b, slice(None), turn_b, mid_b, slice(None))
    base_b = R + S
    for i in range(Z):
        tz = lax.rem(z + i, Z)
        send(5, fwd_b.at[rows_at(tz, G)], rows.at[pl.ds(pl.multiple_of(base_b + z * G, G), G)], (tz * 2 + 1 - core, g))

    wait_recv(2, mark_s.at[pl.ds(0, C - 1)])
    flat[...] = jnp.zeros_like(flat)
    for i in range(C):
        flat[i:i + 1, :] = mark_1[i]
    eye = onehot(iota((16, 128), 0) == iota((16, 128), 1))
    turned = nt(eye, flat[...].astype(BF16))
    for i in range(G):
        mark_2[i] = turned[i:i + 1, :]
    for i in range(1, G):
        tg = lax.rem(g + i, G)
        send(6, mark_2.at[tg], mark_3.at[g], (c, tg))
    mark_3[g] = mark_2[g]

    first_block = gathered_sum(3)
    spread(7, first_block.astype(BF16))

    turn_a = onehot((iota((S, S), 0) & (Z - 1)) * G + lax.div(iota((S, S), 0), Z) == iota((S, S), 1))
    wait_recv(0, mid_a.at[pl.ds(0, S - G)])
    product(fwd_a, slice(None), turn_a, mid_a, slice(None))
    for i in range(1, G):
        tg = lax.rem(g + i, G)
        send(8, fwd_a.at[rows_at(tg, Z)], rows.at[pl.ds(pl.multiple_of(R + g * Z, Z), Z)], (c, tg))
    rows[pl.ds(pl.multiple_of(R + g * Z, Z), Z), :] = fwd_a[rows_at(g, Z), :]

    wait_recv(6, mark_3.at[pl.ds(0, G - 1)])
    for i in range(G):
        flat[i:i + 1, :] = mark_3[i]
    held = flat[0:16, :].astype(BF16)
    alive[:, 0:R] = jnp.where(moving, 0.0, 1.0)
    lane = iota((128, S), 1)
    src = iota((128, S), 0)
    at_a = nn(held, onehot(src == 2 * (lane & (Z - 1)) + core))
    at_b = nn(held, onehot(src == 2 * lax.div(lane, G) + 1 - core))
    lane = iota((16, S), 1)
    src = iota((16, S), 0)
    alive[:, R:R + S] = jnp.sum(jnp.where(lax.div(lane, Z) == src, at_a, 0.0), axis=0, keepdims=True)
    alive[:, R + S:] = jnp.sum(jnp.where((lane & (G - 1)) == src, at_b, 0.0), axis=0, keepdims=True)

    kappa = kappa_ref[0]
    step = S

    def expectation(i):
        at = rows_at(i, step)
        scores = kappa * nt(centres[...], rows[at, :])
        largest = jnp.max(scores, axis=0, keepdims=True)
        powered = jnp.exp(scores - largest)
        summed = jnp.sum(powered, axis=0, keepdims=True)
        here = alive[:, at]
        weights[:, at] = (powered * (1.0 / summed) * here).astype(BF16)
        norms[:, at] = (largest + jnp.log(summed)) * here

    own_steps = R // step
    spread_wait(7)
    pl.loop(0, own_steps)(expectation)
    wait_recv(8, rows.at[pl.ds(0, S - Z)])
    expectation(own_steps)
    wait_recv(5, rows.at[pl.ds(0, S)])
    expectation(own_steps + 1)
    wait_send(3, part.at[pl.ds(0, (G - 1) * kb)])

    half = K // 2
    for it in range(ITERS):
        if it:
            pl.loop(0, own_steps + 2)(expectation)
        for m in range(2):
            product(part, slice(m * half, (m + 1) * half), weights[m * half:(m + 1) * half, :], rows, slice(None))
            scatter(9 + 2 * it, m * G // 2, (m + 1) * G // 2)
        total = gathered_sum(9 + 2 * it)
        length = jnp.sqrt(jnp.sum(total * total, axis=-1, keepdims=True))
        block = (total / jnp.maximum(length, 1.0)).astype(BF16)
        wait_send(7 if it == 0 else 8 + 2 * it, centres.at[pl.ds(0, (G - 1) * kb)])
        spread(10 + 2 * it, block)
        if it == ITERS - 1:
            score_ref[:, 0:R] = norms[:, 0:R]
            lane = iota((S, 2 * S), 1)
            src = iota((S, 2 * S), 0)
            turn = onehot(lane == (src & (Z - 1)) * 2 * G + core * G + lax.div(src, Z))
            moved = nn(split3(norms[:, R:R + S]), turn)
            turn = onehot(lane == lax.div(src, G) * 2 * G + (1 - core) * G + (src & (G - 1)))
            moved = moved + nn(split3(norms[:, R + S:]), turn)
            score_ref[:, R:] = moved[0:1, :] + moved[1:2, :] + moved[2:3, :]
        spread_wait(10 + 2 * it)
        wait_send(9 + 2 * it, part.at[pl.ds(0, (G - 1) * kb)])
    wait_send(10 + 2 * (ITERS - 1), centres.at[pl.ds(0, (G - 1) * kb)])
    cent_ref[...] = centres[...]

    wait_send(0, send_a.at[pl.ds(0, S - G)])
    wait_send(1, send_b.at[pl.ds(0, S - Z)])
    wait_send(2, mark_s.at[pl.ds(0, C - 1)])
    wait_send(5, rows.at[pl.ds(0, S)])
    wait_send(6, mark_3.at[pl.ds(0, G - 1)])
    wait_send(8, rows.at[pl.ds(0, S - Z)])


def shards(embeddings, new_label, dest_member, seed_index, kappa):
    R, D = embeddings.shape
    K = seed_index.shape[1]
    C = lax.axis_size("clusters")
    G = lax.axis_size("group")
    S = C * G // 2
    kb = K // G
    slots = R + 2 * S
    vmem = pl.BlockSpec(memory_space=pltpu.VMEM)
    phases = 10 + 2 * ITERS
    centroids, score = pl.pallas_call(
        functools.partial(kernel, (C, G, R, D, K)),
        name="refine",
        out_shape=(
            jax.ShapeDtypeStruct((K, D), BF16),
            jax.ShapeDtypeStruct((1, slots), F32),
        ),
        in_specs=[vmem, vmem, vmem, vmem, pl.BlockSpec(memory_space=pltpu.SMEM)],
        out_specs=(vmem, vmem),
        scratch_shapes=[
            pltpu.VMEM((slots, D), BF16),
            pltpu.VMEM((max(R, K), max(R, K)), BF16),
            pltpu.VMEM((S, D), BF16),
            pltpu.VMEM((S, D), BF16),
            pltpu.VMEM((S, D), BF16),
            pltpu.VMEM((S, D), BF16),
            pltpu.VMEM((S, D), BF16),
            pltpu.VMEM((S, D), BF16),
            pltpu.VMEM((K, slots), BF16),
            pltpu.VMEM((K, D), BF16),
            pltpu.VMEM((G, kb, D), BF16),
            pltpu.VMEM((kb, D), BF16),
            pltpu.VMEM((K, D), BF16),
            pltpu.VMEM((1, slots), F32),
            pltpu.VMEM((1, slots), F32),
            pltpu.VMEM((C, 1, 128), F32),
            pltpu.VMEM((C, 1, 128), F32),
            pltpu.VMEM((G, 1, 128), F32),
            pltpu.VMEM((G, 1, 128), F32),
            pltpu.VMEM((128, 128), F32),
            pltpu.SemaphoreType.DMA((phases,)),
            pltpu.SemaphoreType.DMA((phases,)),
        ],
        compiler_params=pltpu.CompilerParams(
            collective_id=0, has_side_effects=True, vmem_limit_bytes=40 * 1024 * 1024
        ),
    )(
        embeddings,
        new_label.reshape(1, R),
        dest_member.reshape(1, R),
        seed_index,
        kappa,
    )
    return centroids, score.reshape(slots)


def solution(mesh):
    return jax.shard_map(
        shards,
        mesh=mesh,
        in_specs=(
            P(("clusters", "group"), None),
            P(("clusters", "group")),
            P(("clusters", "group")),
            P("clusters", None),
            P("clusters"),
        ),
        out_specs=(P("clusters", None), P(("clusters", "group"))),
        check_vma=False,
    )
```

time: 432 us -> 149 us (0.34)
  the two profiles are of different devices: /device:TPU:1 before, /device:TPU:100 now
where the time goes in v1:
time: 149 us
  Pallas kernels  143 us (96%)
  local copies, waits for them, and re-layouts  4.14 us (3%)
    pallas_call x1, Pallas kernels, shards(): pl.pallas_call(functools.partial(kernel, (C, G, R, D, K)), name='refine',...  143 us
    unnamed x10, local copies, waits for them, and re-layouts  4.14 us

profile of v1, /device:TPU:100, one launch (start us, length us, event | category | flops | bytes accessed | tf_op | source)
XLA Modules:
  0.0 148.8 jit_solution(300200090617925215)
XLA Ops:
  0.6 0.0 copy-start.2
  1.3 0.0 copy-start.1
  1.3 0.0 copy-done.2
  1.3 0.7 copy-done.1
  2.0 0.0 copy-start
  2.0 1.2 copy-done
  3.2 0.0 copy-start.3
  3.2 0.7 copy-done.3
  3.9 143.3 %refine.1 = (bf16[512,1024]{1,0:T(8,128)(2,1)S(1)}, f32[1,1024]{1,0:T(1,128)S(1)}) custom-call(bf16[512,1024]{1,0:T(8,128)(2,1)S(1)} %copy-done, s32[1,512]{1,0:T(1,128)S(1)} %bitcast.4, s32[1,512]{1,0:T(1,128)S(1)} %bitcast.5, s32[1,512]{1,0:T(1,128)S(1)} %copy-done.3, f32[1]{0:T(128)S(6)} %copy.9.kappa_ref), custom_call_target="tpu_custom_call" | custom-call | tf_op jit(solution)/shard_map/refine/pallas_call | solution.py:278
  147.2 1.0 copy.10
  148.2 0.6 copy.11
Async XLA Ops:
  0.6 0.7 copy-start.2
  1.3 0.7 copy-start.1
  2.0 1.2 copy-start
  3.2 0.7 copy-start.3

commit v2 on v1

--- a/solution.py
+++ b/solution.py
@@ -50,12 +50,13 @@
 
 def kernel(
     dims,
-    x_ref, label_ref, member_ref, seed_ref, kappa_ref,
-    cent_ref, score_ref,
+    x_hbm, label_hbm, member_hbm, seed_hbm, kappa_ref,
+    cent_hbm, score_hbm,
+    x_ref, label_ref, member_ref, seed_ref, score_ref,
     rows, hot, send_a, send_b, mid_a, mid_b, fwd_a, fwd_b,
     weights, part, gather_in, block_out, centres, alive, norms,
     mark_s, mark_1, mark_2, mark_3, flat,
-    send_sem, recv_sem,
+    send_sem, recv_sem, load_sem,
 ):
     C, G, R, D, K = dims
     Z = C // 2
@@ -72,6 +73,15 @@
     for i in range(1, G):
         pl.semaphore_signal(barrier, inc=1, device_id=(c, lax.rem(g + i, G)), device_id_type=MESH)
 
+    loads = [
+        pltpu.make_async_copy(src, dst, load_sem.at[i])
+        for i, (src, dst) in enumerate(
+            ((label_hbm, label_ref), (member_hbm, member_ref), (x_hbm, x_ref), (seed_hbm, seed_ref))
+        )
+    ]
+    for load in loads:
+        load.start()
+
     def send(phase, src, dst, device):
         pltpu.make_async_remote_copy(
             src_ref=src, dst_ref=dst, send_sem=send_sem.at[phase], recv_sem=recv_sem.at[phase],
@@ -92,6 +102,7 @@
             cols = rows_at(j, ncol)
             dst[dst_rows, cols] = nn(lhs, rhs_ref[rhs_rows, cols]).astype(BF16)
 
+    loads[2].wait()
     rstep = min(R, 128)
 
     @pl.loop(0, R // rstep)
@@ -101,6 +112,9 @@
         scale = lax.rsqrt(jnp.sum(v * v, axis=-1, keepdims=True) + EPSILON)
         rows[at, :] = (v * scale).astype(BF16)
 
+    loads[0].wait()
+    loads[1].wait()
+    loads[3].wait()
     label = label_ref[...]
     member = member_ref[...]
     moving = label != c
@@ -110,29 +124,29 @@
     to_b = jnp.where(moving & jnp.logical_not(same), member * Z + lz, -1)
     own = pl.ds(0, R)
 
-    hot[0:S, 0:R] = onehot(iota((S, R), 0) == to_a)
-    product(send_a, slice(None), hot[0:S, 0:R], rows, own)
-    pl.semaphore_wait(barrier, C - 1 + G - 1)
-    for i in range(1, Z):
-        tz = lax.rem(z + i, Z)
-        send(0, send_a.at[rows_at(tz, G)], mid_a.at[rows_at(z, G)], (tz * 2 + core, g))
-    hot[0:S, 0:R] = onehot(iota((S, R), 0) == to_b)
-    product(send_b, slice(None), hot[0:S, 0:R], rows, own)
-    for i in range(1, G):
-        tg = lax.rem(g + i, G)
-        send(1, send_b.at[rows_at(tg, Z)], mid_b.at[rows_at(g, Z)], (c, tg))
-    mid_a[rows_at(z, G), :] = send_a[rows_at(z, G), :]
-    mid_b[rows_at(g, Z), :] = send_b[rows_at(g, Z), :]
-
     to_cluster = onehot((iota((128, R), 0) == label) & moving)
     to_member = onehot(iota((128, R), 0) == member)
     marks = nt(to_cluster, to_member)
     for i in range(C):
         mark_s[i] = marks[i:i + 1, :]
+    mark_1[c] = mark_s[c]
+    hot[0:S, 0:R] = onehot(iota((S, R), 0) == to_a)
+    product(send_a, slice(None), hot[0:S, 0:R], rows, own)
+    hot[0:S, 0:R] = onehot(iota((S, R), 0) == to_b)
+    product(send_b, slice(None), hot[0:S, 0:R], rows, own)
+
+    pl.semaphore_wait(barrier, C - 1 + G - 1)
     for i in range(1, C):
         tc = lax.rem(c + i, C)
         send(2, mark_s.at[tc], mark_1.at[c], (tc, g))
-    mark_1[c] = mark_s[c]
+    for i in range(1, G):
+        tg = lax.rem(g + i, G)
+        send(1, send_b.at[rows_at(tg, Z)], mid_b.at[rows_at(g, Z)], (c, tg))
+    for i in range(1, Z):
+        tz = lax.rem(z + i, Z)
+        send(0, send_a.at[rows_at(tz, G)], mid_a.at[rows_at(z, G)], (tz * 2 + core, g))
+    mid_a[rows_at(z, G), :] = send_a[rows_at(z, G), :]
+    mid_b[rows_at(g, Z), :] = send_b[rows_at(g, Z), :]
 
     hot[0:R, 0:K] = onehot(iota((R, K), 0) + g * R == seed_ref[...])
 
@@ -161,10 +175,9 @@
     def spread_wait(phase):
         wait_recv(phase, centres.at[pl.ds(0, (G - 1) * kb)])
 
-    scatter(3, 0, G)
-
     turn_b = onehot((iota((S, S), 0) & (G - 1)) * Z + lax.div(iota((S, S), 0), G) == iota((S, S), 1))
     wait_recv(1, mid_b.at[pl.ds(0, S - Z)])
+    scatter(3, 0, G)
     product(fwd_b, slice(None), turn_b, mid_b, slice(None))
     base_b = R + S
     for i in range(Z):
@@ -232,6 +245,8 @@
     wait_send(3, part.at[pl.ds(0, (G - 1) * kb)])
 
     half = K // 2
+    put_scores = pltpu.make_async_copy(score_ref, score_hbm, load_sem.at[0])
+    put_centres = pltpu.make_async_copy(centres, cent_hbm, load_sem.at[1])
     for it in range(ITERS):
         if it:
             pl.loop(0, own_steps + 2)(expectation)
@@ -252,10 +267,13 @@
             turn = onehot(lane == lax.div(src, G) * 2 * G + (1 - core) * G + (src & (G - 1)))
             moved = moved + nn(split3(norms[:, R + S:]), turn)
             score_ref[:, R:] = moved[0:1, :] + moved[1:2, :] + moved[2:3, :]
+            put_scores.start()
         spread_wait(10 + 2 * it)
         wait_send(9 + 2 * it, part.at[pl.ds(0, (G - 1) * kb)])
     wait_send(10 + 2 * (ITERS - 1), centres.at[pl.ds(0, (G - 1) * kb)])
-    cent_ref[...] = centres[...]
+    put_centres.start()
+    put_centres.wait()
+    put_scores.wait()
 
     wait_send(0, send_a.at[pl.ds(0, S - G)])
     wait_send(1, send_b.at[pl.ds(0, S - Z)])
@@ -273,7 +291,7 @@
     S = C * G // 2
     kb = K // G
     slots = R + 2 * S
-    vmem = pl.BlockSpec(memory_space=pltpu.VMEM)
+    hbm = pl.BlockSpec(memory_space=pltpu.HBM)
     phases = 10 + 2 * ITERS
     centroids, score = pl.pallas_call(
         functools.partial(kernel, (C, G, R, D, K)),
@@ -282,9 +300,14 @@
             jax.ShapeDtypeStruct((K, D), BF16),
             jax.ShapeDtypeStruct((1, slots), F32),
         ),
-        in_specs=[vmem, vmem, vmem, vmem, pl.BlockSpec(memory_space=pltpu.SMEM)],
-        out_specs=(vmem, vmem),
+        in_specs=[hbm, hbm, hbm, hbm, pl.BlockSpec(memory_space=pltpu.SMEM)],
+        out_specs=(hbm, hbm),
         scratch_shapes=[
+            pltpu.VMEM((R, D), BF16),
+            pltpu.VMEM((1, R), I32),
+            pltpu.VMEM((1, R), I32),
+            pltpu.VMEM((1, K), I32),
+            pltpu.VMEM((1, slots), F32),
             pltpu.VMEM((slots, D), BF16),
             pltpu.VMEM((max(R, K), max(R, K)), BF16),
             pltpu.VMEM((S, D), BF16),
@@ -307,9 +330,10 @@
             pltpu.VMEM((128, 128), F32),
             pltpu.SemaphoreType.DMA((phases,)),
             pltpu.SemaphoreType.DMA((phases,)),
+            pltpu.SemaphoreType.DMA((4,)),
         ],
         compiler_params=pltpu.CompilerParams(
-            collective_id=0, has_side_effects=True, vmem_limit_bytes=40 * 1024 * 1024
+            collective_id=0, has_side_effects=True, vmem_limit_bytes=60 * 1024 * 1024
         ),
     )(
         embeddings,

time: 149 us -> 141 us (0.946)
  the two profiles are of different devices: /device:TPU:100 before, /device:TPU:268 now
where the time goes in v2:
time: 141 us
  Pallas kernels  137 us (97%)
  local copies, waits for them, and re-layouts  2.86 us (2%)
    pallas_call x1, Pallas kernels, shards(): pl.pallas_call(functools.partial(kernel, (C, G, R, D, K)), name='refine',...  137 us
    unnamed x4, local copies, waits for them, and re-layouts  2.86 us

profile of v2, /device:TPU:268, one launch (start us, length us, event | category | flops | bytes accessed | tf_op | source)
XLA Modules:
  0.0 140.8 jit_solution(969297003078651139)
XLA Ops:
  1.3 136.6 %refine.1 = (bf16[512,1024]{1,0:T(8,128)(2,1)}, f32[1,1024]{1,0:T(1,128)}) custom-call(bf16[512,1024]{1,0:T(8,128)(2,1)} %x_hbm.1, s32[1,512]{1,0:T(1,128)} %bitcast.4, s32[1,512]{1,0:T(1,128)} %bitcast.5, s32[1,512]{1,0:T(1,128)} %seed_hbm.1, f32[1]{0:T(128)S(6)} %copy.9.kappa_ref), custom_call_target="tpu_custom_call" | custom-call | tf_op jit(solution)/shard_map/refine/pallas_call | solution.py:296
  137.9 0.0 copy-start
  137.9 2.3 %copy.10 = bf16[512,1024]{1,0:T(8,128)(2,1)} copy(bf16[512,1024]{1,0:T(8,128)(2,1)} %get-tuple-element.8) | data formatting | bytes 2097152
  140.2 0.0 copy-done
  140.2 0.6 copy.11
Async XLA Ops:
  137.9 2.3 %copy-start = (f32[1,1024]{1,0:T(1,128)S(1)}, f32[1,1024]{1,0:T(1,128)}, u32[]{:S(2)}) copy-start(f32[1,1024]{1,0:T(1,128)} %get-tuple-element.5) | copy-start | bytes 12292

commit v3 on v2

--- a/solution.py
+++ b/solution.py
@@ -54,9 +54,9 @@
     cent_hbm, score_hbm,
     x_ref, label_ref, member_ref, seed_ref, score_ref,
     rows, hot, send_a, send_b, mid_a, mid_b, fwd_a, fwd_b,
-    weights, part, gather_in, block_out, centres, alive, norms,
+    weights, part, relay, combined, nearer, line, line_in, centres, alive, norms,
     mark_s, mark_1, mark_2, mark_3, flat,
-    send_sem, recv_sem, load_sem,
+    send_sem, recv_sem, load_sem, plane_send, rs_sem, rs_line_sem, ag_sem, ag_line_sem,
 ):
     C, G, R, D, K = dims
     Z = C // 2
@@ -148,36 +148,151 @@
     mid_a[rows_at(z, G), :] = send_a[rows_at(z, G), :]
     mid_b[rows_at(g, Z), :] = send_b[rows_at(g, Z), :]
 
+    n = round(G ** 0.5)
+    hb = kb // 2
+    Dh = D // 2
+    px, py = g // n, lax.rem(g, n)
+    first = (px, py)
+    second = (py, px)
+    ORDER = (2, 1, 3, 0)
+
+    def at_plane(h, p, o):
+        p, o = lax.rem(p + n, n), lax.rem(o + n, n)
+        return p * n + o if h == 0 else o * n + p
+
+    def block(h, dp, do):
+        return at_plane(h, first[h] + dp, second[h] + do)
+
+    def part_of(b, half=None):
+        if half is None:
+            return pl.ds(pl.multiple_of(b * kb, kb), kb)
+        return pl.ds(pl.multiple_of(b * kb + half * hb, hb), hb)
+
+    def push(phase, src, dst, sem, b):
+        pltpu.make_async_remote_copy(
+            src_ref=src, dst_ref=dst, send_sem=plane_send.at[phase], recv_sem=sem,
+            device_id=(c, b), device_id_type=MESH,
+        ).start()
+
+    def landed(ref, sem):
+        pltpu.make_async_copy(ref, ref, sem).wait()
+
+    def sent(phase):
+        for h in range(2):
+            ref = part.at[h, pl.ds(0, (G - 1) * kb)]
+            pltpu.make_async_copy(ref, ref, plane_send.at[phase]).wait()
+
+    TOP, LOW = pl.ds(0, hb), pl.ds(hb, hb)
+
+    def reduce_scatter(fill):
+        for h in range(2):
+            fill(h)
+            ahead, behind = block(h, 1, 0), block(h, -1, 0)
+            for r in ORDER:
+                far = block(h, 2, r)
+                push(0, part.at[h, part_of(far, 0)], relay.at[h, r, TOP], rs_sem.at[h, r, 0], ahead)
+                push(0, part.at[h, part_of(far, 1)], relay.at[h, r, LOW], rs_sem.at[h, r, 1], behind)
+            for r in ORDER:
+                push(0, part.at[h, part_of(block(h, 1, r), 1)], nearer.at[h, r, 0, LOW], rs_sem.at[h, r, 2], ahead)
+                push(0, part.at[h, part_of(block(h, -1, r), 0)], nearer.at[h, r, 1, TOP], rs_sem.at[h, r, 3], behind)
+        for r in ORDER:
+            for h in range(2):
+                ahead, behind = block(h, 1, 0), block(h, -1, 0)
+                landed(relay.at[h, r, TOP], rs_sem.at[h, r, 0])
+                mine = part[h, part_of(block(h, 1, r), 0), :].astype(F32)
+                combined[h, r, TOP, :] = (mine + relay[h, r, TOP, :].astype(F32)).astype(BF16)
+                push(0, combined.at[h, r, TOP], nearer.at[h, r, 0, TOP], rs_sem.at[h, r, 4], ahead)
+                landed(relay.at[h, r, LOW], rs_sem.at[h, r, 1])
+                mine = part[h, part_of(block(h, -1, r), 1), :].astype(F32)
+                combined[h, r, LOW, :] = (mine + relay[h, r, LOW, :].astype(F32)).astype(BF16)
+                push(0, combined.at[h, r, LOW], nearer.at[h, r, 1, LOW], rs_sem.at[h, r, 5], behind)
+        for r in ORDER:
+            for h in range(2):
+                landed(nearer.at[h, r, 0, LOW], rs_sem.at[h, r, 2])
+                landed(nearer.at[h, r, 1, TOP], rs_sem.at[h, r, 3])
+                landed(nearer.at[h, r, 0, TOP], rs_sem.at[h, r, 4])
+                landed(nearer.at[h, r, 1, LOW], rs_sem.at[h, r, 5])
+                total = part[h, part_of(block(h, 0, r)), :].astype(F32)
+                total = total + nearer[h, r, 0].astype(F32) + nearer[h, r, 1].astype(F32)
+                line[h, r] = total.astype(BF16)
+                if r:
+                    push(0, line.at[h, r], line_in.at[h, r - 1], rs_line_sem.at[h, r - 1], block(h, 0, r))
+        totals = []
+        for h in range(2):
+            total = line[h, 0].astype(F32)
+            for r in range(3):
+                landed(line_in.at[h, r], rs_line_sem.at[h, r])
+                total = total + line_in[h, r].astype(F32)
+            totals.append(total)
+        return totals
+
+    def all_gather(blocks, meanwhile=None):
+        own_at = part_of(g)
+        for h in range(2):
+            centres[h, own_at, :] = blocks[h]
+
+        def along(h, r):
+            here = part_of(block(h, 0, r))
+            push(1, centres.at[h, here], centres.at[h, here], ag_sem.at[h, r, 0], block(h, 1, 0))
+            push(1, centres.at[h, here], centres.at[h, here], ag_sem.at[h, r, 1], block(h, -1, 0))
+            if r == 2:
+                push(1, centres.at[h, here], centres.at[h, here], ag_sem.at[h, r, 2], block(h, 2, 0))
+
+        def forward(h, r):
+            back, front = block(h, -1, r), block(h, 1, r)
+            landed(centres.at[h, part_of(back)], ag_sem.at[h, r, 0])
+            if r != 2:
+                top = part_of(back, 0)
+                push(1, centres.at[h, top], centres.at[h, top], ag_sem.at[h, r, 2], block(h, 1, 0))
+            landed(centres.at[h, part_of(front)], ag_sem.at[h, r, 1])
+            if r != 2:
+                low = part_of(front, 1)
+                push(1, centres.at[h, low], centres.at[h, low], ag_sem.at[h, r, 3], block(h, -1, 0))
+
+        for h in range(2):
+            for r in (1, 3, 2):
+                push(1, centres.at[h, own_at], centres.at[h, own_at], ag_line_sem.at[h, r - 1], block(h, 0, r))
+            along(h, 0)
+        if meanwhile is not None:
+            meanwhile()
+        for r in (3, 1):
+            for h in range(2):
+                landed(centres.at[h, part_of(block(h, 0, r))], ag_line_sem.at[h, n - r - 1])
+                along(h, r)
+        for h in range(2):
+            forward(h, 0)
+        for h in range(2):
+            landed(centres.at[h, part_of(block(h, 0, 2))], ag_line_sem.at[h, 1])
+            along(h, 2)
+        for r in (3, 1, 2):
+            for h in range(2):
+                forward(h, r)
+        for r in (0, 3, 1, 2):
+            for h in range(2):
+                far = block(h, 2, r)
+                if r == 2:
+                    landed(centres.at[h, part_of(far)], ag_sem.at[h, r, 2])
+                else:
+                    landed(centres.at[h, part_of(far, 0)], ag_sem.at[h, r, 2])
+                    landed(centres.at[h, part_of(far, 1)], ag_sem.at[h, r, 3])
+
     hot[0:R, 0:K] = onehot(iota((R, K), 0) + g * R == seed_ref[...])
-
-    @pl.loop(0, D // ncol)
-    def _(j):
-        cols = rows_at(j, ncol)
-        part[:, cols] = tn(hot[0:R, 0:K], rows[own, cols]).astype(BF16)
-
-    def scatter(phase, first, last):
-        for b in range(first, last):
-            @pl.when(b != g)
-            def _():
-                send(phase, part.at[pl.ds(b * kb, kb)], gather_in.at[g], (c, b))
-
-    def gathered_sum(phase):
-        wait_recv(phase, gather_in.at[pl.ds(0, G - 1)])
-        gather_in[g] = part[rows_at(g, kb), :]
-        return jnp.sum(gather_in[...].astype(F32), axis=0)
-
-    def spread(phase, block):
-        block_out[...] = block
-        for i in range(1, G):
-            send(phase, block_out, centres.at[rows_at(g, kb)], (c, lax.rem(g + i, G)))
-        centres[rows_at(g, kb), :] = block
-
-    def spread_wait(phase):
-        wait_recv(phase, centres.at[pl.ds(0, (G - 1) * kb)])
+    hcol = min(Dh, 256)
+
+    def fill_seeds(h):
+        @pl.loop(0, Dh // hcol)
+        def _(j):
+            cols = pl.ds(pl.multiple_of(h * Dh + j * hcol, hcol), hcol)
+            part[h, :, rows_at(j, hcol)] = tn(hot[0:R, 0:K], rows[own, cols]).astype(BF16)
+
+    def fill_sums(h):
+        @pl.loop(0, Dh // hcol)
+        def _(j):
+            cols = pl.ds(pl.multiple_of(h * Dh + j * hcol, hcol), hcol)
+            part[h, :, rows_at(j, hcol)] = nn(weights[...], rows[:, cols]).astype(BF16)
 
     turn_b = onehot((iota((S, S), 0) & (G - 1)) * Z + lax.div(iota((S, S), 0), G) == iota((S, S), 1))
     wait_recv(1, mid_b.at[pl.ds(0, S - Z)])
-    scatter(3, 0, G)
     product(fwd_b, slice(None), turn_b, mid_b, slice(None))
     base_b = R + S
     for i in range(Z):
@@ -197,8 +312,9 @@
         send(6, mark_2.at[tg], mark_3.at[g], (c, tg))
     mark_3[g] = mark_2[g]
 
-    first_block = gathered_sum(3)
-    spread(7, first_block.astype(BF16))
+    all_gather([t.astype(BF16) for t in reduce_scatter(fill_seeds)])
+    sent(0)
+    sent(1)
 
     turn_a = onehot((iota((S, S), 0) & (Z - 1)) * G + lax.div(iota((S, S), 0), Z) == iota((S, S), 1))
     wait_recv(0, mid_a.at[pl.ds(0, S - G)])
@@ -227,7 +343,8 @@
 
     def expectation(i):
         at = rows_at(i, step)
-        scores = kappa * nt(centres[...], rows[at, :])
+        scores = nt(centres[0], rows[at, 0:Dh]) + nt(centres[1], rows[at, Dh:D])
+        scores = kappa * scores
         largest = jnp.max(scores, axis=0, keepdims=True)
         powered = jnp.exp(scores - largest)
         summed = jnp.sum(powered, axis=0, keepdims=True)
@@ -236,43 +353,41 @@
         norms[:, at] = (largest + jnp.log(summed)) * here
 
     own_steps = R // step
-    spread_wait(7)
     pl.loop(0, own_steps)(expectation)
     wait_recv(8, rows.at[pl.ds(0, S - Z)])
     expectation(own_steps)
     wait_recv(5, rows.at[pl.ds(0, S)])
     expectation(own_steps + 1)
-    wait_send(3, part.at[pl.ds(0, (G - 1) * kb)])
-
-    half = K // 2
     put_scores = pltpu.make_async_copy(score_ref, score_hbm, load_sem.at[0])
-    put_centres = pltpu.make_async_copy(centres, cent_hbm, load_sem.at[1])
+
+    def place_scores():
+        score_ref[:, 0:R] = norms[:, 0:R]
+        lane = iota((S, 2 * S), 1)
+        src = iota((S, 2 * S), 0)
+        turn = onehot(lane == (src & (Z - 1)) * 2 * G + core * G + lax.div(src, Z))
+        moved = nn(split3(norms[:, R:R + S]), turn)
+        turn = onehot(lane == lax.div(src, G) * 2 * G + (1 - core) * G + (src & (G - 1)))
+        moved = moved + nn(split3(norms[:, R + S:]), turn)
+        score_ref[:, R:] = moved[0:1, :] + moved[1:2, :] + moved[2:3, :]
+        put_scores.start()
+
     for it in range(ITERS):
         if it:
             pl.loop(0, own_steps + 2)(expectation)
-        for m in range(2):
-            product(part, slice(m * half, (m + 1) * half), weights[m * half:(m + 1) * half, :], rows, slice(None))
-            scatter(9 + 2 * it, m * G // 2, (m + 1) * G // 2)
-        total = gathered_sum(9 + 2 * it)
-        length = jnp.sqrt(jnp.sum(total * total, axis=-1, keepdims=True))
-        block = (total / jnp.maximum(length, 1.0)).astype(BF16)
-        wait_send(7 if it == 0 else 8 + 2 * it, centres.at[pl.ds(0, (G - 1) * kb)])
-        spread(10 + 2 * it, block)
-        if it == ITERS - 1:
-            score_ref[:, 0:R] = norms[:, 0:R]
-            lane = iota((S, 2 * S), 1)
-            src = iota((S, 2 * S), 0)
-            turn = onehot(lane == (src & (Z - 1)) * 2 * G + core * G + lax.div(src, Z))
-            moved = nn(split3(norms[:, R:R + S]), turn)
-            turn = onehot(lane == lax.div(src, G) * 2 * G + (1 - core) * G + (src & (G - 1)))
-            moved = moved + nn(split3(norms[:, R + S:]), turn)
-            score_ref[:, R:] = moved[0:1, :] + moved[1:2, :] + moved[2:3, :]
-            put_scores.start()
-        spread_wait(10 + 2 * it)
-        wait_send(9 + 2 * it, part.at[pl.ds(0, (G - 1) * kb)])
-    wait_send(10 + 2 * (ITERS - 1), centres.at[pl.ds(0, (G - 1) * kb)])
-    put_centres.start()
-    put_centres.wait()
+        totals = reduce_scatter(fill_sums)
+        squares = [jnp.sum(t * t, axis=-1, keepdims=True) for t in totals]
+        length = jnp.maximum(jnp.sqrt(squares[0] + squares[1]), 1.0)
+        all_gather([(t / length).astype(BF16) for t in totals], place_scores if it == ITERS - 1 else None)
+        sent(0)
+        sent(1)
+    puts = [
+        pltpu.make_async_copy(centres.at[h], cent_hbm.at[:, pl.ds(h * Dh, Dh)], load_sem.at[1 + h])
+        for h in range(2)
+    ]
+    for put in puts:
+        put.start()
+    for put in puts:
+        put.wait()
     put_scores.wait()
 
     wait_send(0, send_a.at[pl.ds(0, S - G)])
@@ -292,7 +407,7 @@
     kb = K // G
     slots = R + 2 * S
     hbm = pl.BlockSpec(memory_space=pltpu.HBM)
-    phases = 10 + 2 * ITERS
+    phases = 9
     centroids, score = pl.pallas_call(
         functools.partial(kernel, (C, G, R, D, K)),
         name="refine",
@@ -317,10 +432,13 @@
             pltpu.VMEM((S, D), BF16),
             pltpu.VMEM((S, D), BF16),
             pltpu.VMEM((K, slots), BF16),
-            pltpu.VMEM((K, D), BF16),
-            pltpu.VMEM((G, kb, D), BF16),
-            pltpu.VMEM((kb, D), BF16),
-            pltpu.VMEM((K, D), BF16),
+            pltpu.VMEM((2, K, D // 2), BF16),
+            pltpu.VMEM((2, 4, kb, D // 2), BF16),
+            pltpu.VMEM((2, 4, kb, D // 2), BF16),
+            pltpu.VMEM((2, 4, 2, kb, D // 2), BF16),
+            pltpu.VMEM((2, 4, kb, D // 2), BF16),
+            pltpu.VMEM((2, 3, kb, D // 2), BF16),
+            pltpu.VMEM((2, K, D // 2), BF16),
             pltpu.VMEM((1, slots), F32),
             pltpu.VMEM((1, slots), F32),
             pltpu.VMEM((C, 1, 128), F32),
@@ -331,6 +449,11 @@
             pltpu.SemaphoreType.DMA((phases,)),
             pltpu.SemaphoreType.DMA((phases,)),
             pltpu.SemaphoreType.DMA((4,)),
+            pltpu.SemaphoreType.DMA((2,)),
+            pltpu.SemaphoreType.DMA((2, 4, 6)),
+            pltpu.SemaphoreType.DMA((2, 3)),
+            pltpu.SemaphoreType.DMA((2, 4, 4)),
+            pltpu.SemaphoreType.DMA((2, 3)),
         ],
         compiler_params=pltpu.CompilerParams(
             collective_id=0, has_side_effects=True, vmem_limit_bytes=60 * 1024 * 1024

time: 141 us -> 122 us (0.87)
  the two profiles are of different devices: /device:TPU:268 before, /device:TPU:64 now
where the time goes in v3:
time: 122 us
  Pallas kernels  118 us (97%)
  local copies, waits for them, and re-layouts  2.86 us (2%)
  between operations  1.29 us (1%)
    pallas_call x1, Pallas kernels, shards(): pl.pallas_call(functools.partial(kernel, (C, G, R, D, K)), name='refine',...  118 us
    unnamed x4, local copies, waits for them, and re-layouts  2.86 us

profile of v3, /device:TPU:64, one launch (start us, length us, event | category | flops | bytes accessed | tf_op | source)
XLA Modules:
  0.0 122.3 jit_solution(2575084476557296423)
XLA Ops:
  1.3 118.1 %refine.1 = (bf16[512,1024]{1,0:T(8,128)(2,1)}, f32[1,1024]{1,0:T(1,128)}) custom-call(bf16[512,1024]{1,0:T(8,128)(2,1)} %x_hbm.1, s32[1,512]{1,0:T(1,128)} %bitcast.4, s32[1,512]{1,0:T(1,128)} %bitcast.5, s32[1,512]{1,0:T(1,128)} %seed_hbm.1, f32[1]{0:T(128)S(6)} %copy.9.kappa_ref), custom_call_target="tpu_custom_call" | custom-call | tf_op jit(solution)/shard_map/refine/pallas_call | solution.py:411
  119.4 0.0 copy-start
  119.4 2.3 %copy.10 = bf16[512,1024]{1,0:T(8,128)(2,1)} copy(bf16[512,1024]{1,0:T(8,128)(2,1)} %get-tuple-element.8) | data formatting | bytes 2097152
  121.7 0.0 copy-done
  121.7 0.6 copy.11
Async XLA Ops:
  119.4 2.3 %copy-start = (f32[1,1024]{1,0:T(1,128)S(1)}, f32[1,1024]{1,0:T(1,128)}, u32[]{:S(2)}) copy-start(f32[1,1024]{1,0:T(1,128)} %get-tuple-element.5) | copy-start | bytes 12292

commit v4 on v3

--- a/solution.py
+++ b/solution.py
@@ -50,13 +50,13 @@
 
 def kernel(
     dims,
-    x_hbm, label_hbm, member_hbm, seed_hbm, kappa_ref,
-    cent_hbm, score_hbm,
-    x_ref, label_ref, member_ref, seed_ref, score_ref,
+    x_hbm, label_hbm, member_hbm, seed_hbm, kappa_hbm,
+    cent_ref, score_ref,
+    x_ref, label_ref, member_ref, seed_ref, kappa_ref,
     rows, hot, send_a, send_b, mid_a, mid_b, fwd_a, fwd_b,
     weights, part, relay, combined, nearer, line, line_in, centres, alive, norms,
     mark_s, mark_1, mark_2, mark_3, flat,
-    send_sem, recv_sem, load_sem, plane_send, rs_sem, rs_line_sem, ag_sem, ag_line_sem,
+    send_sem, recv_sem, load_sem, ready, plane_send, rs_sem, rs_line_sem, ag_sem, ag_line_sem,
 ):
     C, G, R, D, K = dims
     Z = C // 2
@@ -68,18 +68,27 @@
     core = lax.rem(c, 2)
 
     barrier = pltpu.get_barrier_semaphore()
-    for i in range(1, C):
-        pl.semaphore_signal(barrier, inc=1, device_id=(lax.rem(c + i, C), g), device_id_type=MESH)
+    for i in range(1, Z):
+        pl.semaphore_signal(barrier, inc=1, device_id=(lax.rem(z + i, Z) * 2 + core, g), device_id_type=MESH)
     for i in range(1, G):
         pl.semaphore_signal(barrier, inc=1, device_id=(c, lax.rem(g + i, G)), device_id_type=MESH)
 
+    @pl.when(core == 0)
+    def _():
+        for i in range(Z):
+            pl.semaphore_signal(barrier, inc=1, device_id=(lax.rem(z + i, Z) * 2 + 1, g), device_id_type=MESH)
+
+    chunks = 4
+    rstep = R // chunks
     loads = [
+        pltpu.make_async_copy(x_hbm.at[pl.ds(i * rstep, rstep)], x_ref.at[pl.ds(i * rstep, rstep)], load_sem.at[4 + i])
+        for i in range(chunks)
+    ]
+    small = [
         pltpu.make_async_copy(src, dst, load_sem.at[i])
-        for i, (src, dst) in enumerate(
-            ((label_hbm, label_ref), (member_hbm, member_ref), (x_hbm, x_ref), (seed_hbm, seed_ref))
-        )
+        for i, (src, dst) in enumerate(((label_hbm, label_ref), (member_hbm, member_ref), (seed_hbm, seed_ref), (kappa_hbm, kappa_ref)))
     ]
-    for load in loads:
+    for load in loads + small:
         load.start()
 
     def send(phase, src, dst, device):
@@ -102,51 +111,44 @@
             cols = rows_at(j, ncol)
             dst[dst_rows, cols] = nn(lhs, rhs_ref[rhs_rows, cols]).astype(BF16)
 
-    loads[2].wait()
-    rstep = min(R, 128)
-
-    @pl.loop(0, R // rstep)
-    def _(i):
-        at = rows_at(i, rstep)
+    for i in range(chunks):
+        loads[i].wait()
+        at = pl.ds(i * rstep, rstep)
         v = x_ref[at, :].astype(F32)
         scale = lax.rsqrt(jnp.sum(v * v, axis=-1, keepdims=True) + EPSILON)
         rows[at, :] = (v * scale).astype(BF16)
-
-    loads[0].wait()
-    loads[1].wait()
-    loads[3].wait()
+    for load in small:
+        load.wait()
     label = label_ref[...]
     member = member_ref[...]
     moving = label != c
     lz = lax.shift_right_logical(label, 1)
-    same = (label & 1) == core
-    to_a = jnp.where(moving & same, lz * G + member, -1)
-    to_b = jnp.where(moving & jnp.logical_not(same), member * Z + lz, -1)
+    side = label & 1
     own = pl.ds(0, R)
 
-    to_cluster = onehot((iota((128, R), 0) == label) & moving)
-    to_member = onehot(iota((128, R), 0) == member)
-    marks = nt(to_cluster, to_member)
-    for i in range(C):
-        mark_s[i] = marks[i:i + 1, :]
-    mark_1[c] = mark_s[c]
-    hot[0:S, 0:R] = onehot(iota((S, R), 0) == to_a)
+    hot[0:S, 0:R] = onehot(iota((S, R), 0) == jnp.where(moving & (side == 0), lz * G + member, -1))
     product(send_a, slice(None), hot[0:S, 0:R], rows, own)
-    hot[0:S, 0:R] = onehot(iota((S, R), 0) == to_b)
-    product(send_b, slice(None), hot[0:S, 0:R], rows, own)
-
-    pl.semaphore_wait(barrier, C - 1 + G - 1)
-    for i in range(1, C):
-        tc = lax.rem(c + i, C)
-        send(2, mark_s.at[tc], mark_1.at[c], (tc, g))
-    for i in range(1, G):
-        tg = lax.rem(g + i, G)
-        send(1, send_b.at[rows_at(tg, Z)], mid_b.at[rows_at(g, Z)], (c, tg))
-    for i in range(1, Z):
-        tz = lax.rem(z + i, Z)
-        send(0, send_a.at[rows_at(tz, G)], mid_a.at[rows_at(z, G)], (tz * 2 + core, g))
-    mid_a[rows_at(z, G), :] = send_a[rows_at(z, G), :]
-    mid_b[rows_at(g, Z), :] = send_b[rows_at(g, Z), :]
+
+    pl.semaphore_wait(barrier, Z - 1 + G - 1 + core * Z)
+
+    @pl.when(core == 0)
+    def _():
+        for i in range(1, Z):
+            tz = lax.rem(z + i, Z)
+            send(0, send_a.at[rows_at(tz, G)], mid_a.at[0, rows_at(z, G)], (tz * 2, g))
+        mid_a[0, rows_at(z, G), :] = send_a[rows_at(z, G), :]
+
+    @pl.when(core == 1)
+    def _():
+        for i in range(Z):
+            tz = lax.rem(z + i, Z)
+            pl.semaphore_signal(ready, inc=1, device_id=(tz * 2, g), device_id_type=MESH)
+            send(3, send_a.at[rows_at(tz, G)], mid_a.at[1, rows_at(z, G)], (tz * 2, g))
+
+    def cross_marks():
+        for i in range(Z):
+            tc = lax.rem(z + i, Z) * 2 + 1 - core
+            send(4, mark_s.at[tc], mark_1.at[c], (tc, g))
 
     n = round(G ** 0.5)
     hb = kb // 2
@@ -184,7 +186,7 @@
 
     TOP, LOW = pl.ds(0, hb), pl.ds(hb, hb)
 
-    def reduce_scatter(fill):
+    def reduce_scatter(fill, meanwhile=None):
         for h in range(2):
             fill(h)
             ahead, behind = block(h, 1, 0), block(h, -1, 0)
@@ -195,6 +197,8 @@
             for r in ORDER:
                 push(0, part.at[h, part_of(block(h, 1, r), 1)], nearer.at[h, r, 0, LOW], rs_sem.at[h, r, 2], ahead)
                 push(0, part.at[h, part_of(block(h, -1, r), 0)], nearer.at[h, r, 1, TOP], rs_sem.at[h, r, 3], behind)
+        if meanwhile is not None:
+            meanwhile()
         for r in ORDER:
             for h in range(2):
                 ahead, behind = block(h, 1, 0), block(h, -1, 0)
@@ -226,7 +230,7 @@
             totals.append(total)
         return totals
 
-    def all_gather(blocks, meanwhile=None):
+    def all_gather(blocks, meanwhile=None, midway=None):
         own_at = part_of(g)
         for h in range(2):
             centres[h, own_at, :] = blocks[h]
@@ -252,6 +256,7 @@
         for h in range(2):
             for r in (1, 3, 2):
                 push(1, centres.at[h, own_at], centres.at[h, own_at], ag_line_sem.at[h, r - 1], block(h, 0, r))
+        for h in range(2):
             along(h, 0)
         if meanwhile is not None:
             meanwhile()
@@ -264,6 +269,8 @@
         for h in range(2):
             landed(centres.at[h, part_of(block(h, 0, 2))], ag_line_sem.at[h, 1])
             along(h, 2)
+        if midway is not None:
+            midway()
         for r in (3, 1, 2):
             for h in range(2):
                 forward(h, r)
@@ -291,15 +298,58 @@
             cols = pl.ds(pl.multiple_of(h * Dh + j * hcol, hcol), hcol)
             part[h, :, rows_at(j, hcol)] = nn(weights[...], rows[:, cols]).astype(BF16)
 
-    turn_b = onehot((iota((S, S), 0) & (G - 1)) * Z + lax.div(iota((S, S), 0), G) == iota((S, S), 1))
-    wait_recv(1, mid_b.at[pl.ds(0, S - Z)])
-    product(fwd_b, slice(None), turn_b, mid_b, slice(None))
-    base_b = R + S
-    for i in range(Z):
-        tz = lax.rem(z + i, Z)
-        send(5, fwd_b.at[rows_at(tz, G)], rows.at[pl.ds(pl.multiple_of(base_b + z * G, G), G)], (tz * 2 + 1 - core, g))
-
-    wait_recv(2, mark_s.at[pl.ds(0, C - 1)])
+    def other_rows():
+        hot[0:S, 0:R] = onehot(iota((S, R), 0) == jnp.where(moving & (side == 1), member * Z + lz, -1))
+        product(send_b, slice(None), hot[0:S, 0:R], rows, own)
+        mid_b[rows_at(g, Z), :] = send_b[rows_at(g, Z), :]
+        to_cluster = onehot((iota((128, R), 0) == label) & moving)
+        to_member = onehot(iota((128, R), 0) == member)
+        marks = nt(to_cluster, to_member)
+        for i in range(C):
+            mark_s[i] = marks[i:i + 1, :]
+        mark_1[c] = mark_s[c]
+        for i in range(1, Z):
+            tc = lax.rem(z + i, Z) * 2 + core
+            send(2, mark_s.at[tc], mark_1.at[c], (tc, g))
+        pl.when(core == 1)(cross_marks)
+
+    def other_sends():
+        for i in range(1, G):
+            tg = lax.rem(g + i, G)
+            send(1, send_b.at[rows_at(tg, Z)], mid_b.at[rows_at(g, Z)], (c, tg))
+
+        @pl.when(core == 0)
+        def _():
+            pl.semaphore_wait(ready, Z)
+            cross_marks()
+
+    landing = rows.at[pl.ds(pl.multiple_of(R + core * S + z * G, G), G)]
+
+    def other_legs():
+        turn_b = onehot((iota((S, S), 0) & (G - 1)) * Z + lax.div(iota((S, S), 0), G) == iota((S, S), 1))
+        wait_recv(1, mid_b.at[pl.ds(0, S - Z)])
+        product(fwd_b, slice(None), turn_b, mid_b, slice(None))
+
+        @pl.when(core == 1)
+        def _():
+            for i in range(1, Z):
+                tz = lax.rem(z + i, Z)
+                send(5, fwd_b.at[rows_at(tz, G)], landing, (tz * 2 + 1, g))
+            landing[...] = fwd_b[rows_at(z, G), :]
+
+        @pl.when(core == 0)
+        def _():
+            for i in range(Z):
+                tz = lax.rem(z + i, Z)
+                send(6, fwd_b.at[rows_at(tz, G)], landing, (tz * 2 + 1, g))
+
+    first_blocks = [t.astype(BF16) for t in reduce_scatter(fill_seeds, other_rows)]
+    all_gather(first_blocks, other_sends, other_legs)
+    sent(0)
+    sent(1)
+
+    wait_recv(2, mark_s.at[pl.ds(0, Z - 1)])
+    wait_recv(4, mark_s.at[pl.ds(0, Z)])
     flat[...] = jnp.zeros_like(flat)
     for i in range(C):
         flat[i:i + 1, :] = mark_1[i]
@@ -309,34 +359,38 @@
         mark_2[i] = turned[i:i + 1, :]
     for i in range(1, G):
         tg = lax.rem(g + i, G)
-        send(6, mark_2.at[tg], mark_3.at[g], (c, tg))
+        send(9, mark_2.at[tg], mark_3.at[g], (c, tg))
     mark_3[g] = mark_2[g]
 
-    all_gather([t.astype(BF16) for t in reduce_scatter(fill_seeds)])
-    sent(0)
-    sent(1)
-
     turn_a = onehot((iota((S, S), 0) & (Z - 1)) * G + lax.div(iota((S, S), 0), Z) == iota((S, S), 1))
-    wait_recv(0, mid_a.at[pl.ds(0, S - G)])
-    product(fwd_a, slice(None), turn_a, mid_a, slice(None))
-    for i in range(1, G):
-        tg = lax.rem(g + i, G)
-        send(8, fwd_a.at[rows_at(tg, Z)], rows.at[pl.ds(pl.multiple_of(R + g * Z, Z), Z)], (c, tg))
-    rows[pl.ds(pl.multiple_of(R + g * Z, Z), Z), :] = fwd_a[rows_at(g, Z), :]
-
-    wait_recv(6, mark_3.at[pl.ds(0, G - 1)])
-    for i in range(G):
-        flat[i:i + 1, :] = mark_3[i]
-    held = flat[0:16, :].astype(BF16)
+
+    def second_leg(part_a, phase):
+        at = pl.ds(pl.multiple_of(R + part_a * S + g * Z, Z), Z)
+
+        @pl.loop(0, D // ncol)
+        def _(j):
+            cols = rows_at(j, ncol)
+            fwd_a[part_a, :, cols] = nn(turn_a, mid_a[part_a, :, cols]).astype(BF16)
+
+        for i in range(1, G):
+            tg = lax.rem(g + i, G)
+            send(phase, fwd_a.at[part_a, rows_at(tg, Z)], rows.at[at], (c, tg))
+        rows[at, :] = fwd_a[part_a, rows_at(g, Z), :]
+
+    @pl.when(core == 0)
+    def _():
+        wait_recv(0, mid_a.at[0, pl.ds(0, S - G)])
+        second_leg(0, 8)
+        wait_recv(3, mid_a.at[1])
+        second_leg(1, 7)
+
     alive[:, 0:R] = jnp.where(moving, 0.0, 1.0)
-    lane = iota((128, S), 1)
-    src = iota((128, S), 0)
-    at_a = nn(held, onehot(src == 2 * (lane & (Z - 1)) + core))
-    at_b = nn(held, onehot(src == 2 * lax.div(lane, G) + 1 - core))
-    lane = iota((16, S), 1)
-    src = iota((16, S), 0)
-    alive[:, R:R + S] = jnp.sum(jnp.where(lax.div(lane, Z) == src, at_a, 0.0), axis=0, keepdims=True)
-    alive[:, R + S:] = jnp.sum(jnp.where((lane & (G - 1)) == src, at_b, 0.0), axis=0, keepdims=True)
+
+    def origin(index):
+        q = index & (S - 1)
+        from_z = (1 - core) * (q & (Z - 1)) + core * lax.div(q, G)
+        from_g = (1 - core) * lax.div(q, Z) + core * (q & (G - 1))
+        return 2 * from_z + lax.div(index, S), from_g
 
     kappa = kappa_ref[0]
     step = S
@@ -354,22 +408,40 @@
 
     own_steps = R // step
     pl.loop(0, own_steps)(expectation)
-    wait_recv(8, rows.at[pl.ds(0, S - Z)])
-    expectation(own_steps)
-    wait_recv(5, rows.at[pl.ds(0, S)])
-    expectation(own_steps + 1)
-    put_scores = pltpu.make_async_copy(score_ref, score_hbm, load_sem.at[0])
+
+    wait_recv(9, mark_3.at[pl.ds(0, G - 1)])
+    for i in range(G):
+        flat[i:i + 1, :] = mark_3[i]
+    from_c, from_g = origin(iota((1, 2 * S), 1))
+    held = nn(flat[0:16, :].astype(BF16), onehot(iota((128, 2 * S), 0) == from_c))
+    alive[:, R:] = jnp.sum(jnp.where(iota((16, 2 * S), 0) == from_g, held, 0.0), axis=0, keepdims=True)
+
+    @pl.when(core == 0)
+    def _():
+        wait_recv(8, rows.at[pl.ds(0, S - Z)])
+
+    @pl.when(core == 1)
+    def _():
+        wait_recv(5, rows.at[pl.ds(0, S - G)])
+
+    expectation(own_steps + core)
+
+    @pl.when(core == 0)
+    def _():
+        wait_recv(7, rows.at[pl.ds(0, S - Z)])
+
+    @pl.when(core == 1)
+    def _():
+        wait_recv(6, rows.at[pl.ds(0, S)])
+
+    expectation(own_steps + 1 - core)
 
     def place_scores():
         score_ref[:, 0:R] = norms[:, 0:R]
-        lane = iota((S, 2 * S), 1)
-        src = iota((S, 2 * S), 0)
-        turn = onehot(lane == (src & (Z - 1)) * 2 * G + core * G + lax.div(src, Z))
-        moved = nn(split3(norms[:, R:R + S]), turn)
-        turn = onehot(lane == lax.div(src, G) * 2 * G + (1 - core) * G + (src & (G - 1)))
-        moved = moved + nn(split3(norms[:, R + S:]), turn)
+        from_c, from_g = origin(iota((2 * S, 1), 0))
+        turn = onehot(iota((2 * S, 2 * S), 1) == from_c * G + from_g)
+        moved = nn(split3(norms[:, R:]), turn)
         score_ref[:, R:] = moved[0:1, :] + moved[1:2, :] + moved[2:3, :]
-        put_scores.start()
 
     for it in range(ITERS):
         if it:
@@ -380,22 +452,25 @@
         all_gather([(t / length).astype(BF16) for t in totals], place_scores if it == ITERS - 1 else None)
         sent(0)
         sent(1)
-    puts = [
-        pltpu.make_async_copy(centres.at[h], cent_hbm.at[:, pl.ds(h * Dh, Dh)], load_sem.at[1 + h])
-        for h in range(2)
-    ]
-    for put in puts:
-        put.start()
-    for put in puts:
-        put.wait()
-    put_scores.wait()
-
-    wait_send(0, send_a.at[pl.ds(0, S - G)])
+    cent_ref[:, 0:Dh] = centres[0]
+    cent_ref[:, Dh:D] = centres[1]
+
     wait_send(1, send_b.at[pl.ds(0, S - Z)])
-    wait_send(2, mark_s.at[pl.ds(0, C - 1)])
-    wait_send(5, rows.at[pl.ds(0, S)])
-    wait_send(6, mark_3.at[pl.ds(0, G - 1)])
-    wait_send(8, rows.at[pl.ds(0, S - Z)])
+    wait_send(2, mark_s.at[pl.ds(0, Z - 1)])
+    wait_send(4, mark_s.at[pl.ds(0, Z)])
+    wait_send(9, mark_3.at[pl.ds(0, G - 1)])
+
+    @pl.when(core == 0)
+    def _():
+        wait_send(0, send_a.at[pl.ds(0, S - G)])
+        wait_send(6, rows.at[pl.ds(0, S)])
+        wait_send(7, rows.at[pl.ds(0, S - Z)])
+        wait_send(8, rows.at[pl.ds(0, S - Z)])
+
+    @pl.when(core == 1)
+    def _():
+        wait_send(3, rows.at[pl.ds(0, S)])
+        wait_send(5, rows.at[pl.ds(0, S - G)])
 
 
 def shards(embeddings, new_label, dest_member, seed_index, kappa):
@@ -407,29 +482,30 @@
     kb = K // G
     slots = R + 2 * S
     hbm = pl.BlockSpec(memory_space=pltpu.HBM)
-    phases = 9
+    vmem = pl.BlockSpec(memory_space=pltpu.VMEM)
+    phases = 10
     centroids, score = pl.pallas_call(
         functools.partial(kernel, (C, G, R, D, K)),
         name="refine",
         out_shape=(
-            jax.ShapeDtypeStruct((K, D), BF16),
-            jax.ShapeDtypeStruct((1, slots), F32),
+            pltpu.VMEM((K, D), BF16),
+            pltpu.VMEM((1, slots), F32),
         ),
-        in_specs=[hbm, hbm, hbm, hbm, pl.BlockSpec(memory_space=pltpu.SMEM)],
-        out_specs=(hbm, hbm),
+        in_specs=[hbm] * 5,
+        out_specs=(vmem, vmem),
         scratch_shapes=[
             pltpu.VMEM((R, D), BF16),
             pltpu.VMEM((1, R), I32),
             pltpu.VMEM((1, R), I32),
             pltpu.VMEM((1, K), I32),
-            pltpu.VMEM((1, slots), F32),
+            pltpu.SMEM((1,), F32),
             pltpu.VMEM((slots, D), BF16),
             pltpu.VMEM((max(R, K), max(R, K)), BF16),
             pltpu.VMEM((S, D), BF16),
             pltpu.VMEM((S, D), BF16),
+            pltpu.VMEM((2, S, D), BF16),
             pltpu.VMEM((S, D), BF16),
-            pltpu.VMEM((S, D), BF16),
-            pltpu.VMEM((S, D), BF16),
+            pltpu.VMEM((2, S, D), BF16),
             pltpu.VMEM((S, D), BF16),
             pltpu.VMEM((K, slots), BF16),
             pltpu.VMEM((2, K, D // 2), BF16),
@@ -448,7 +524,8 @@
             pltpu.VMEM((128, 128), F32),
             pltpu.SemaphoreType.DMA((phases,)),
             pltpu.SemaphoreType.DMA((phases,)),
-            pltpu.SemaphoreType.DMA((4,)),
+            pltpu.SemaphoreType.DMA((8,)),
+            pltpu.SemaphoreType.REGULAR,
             pltpu.SemaphoreType.DMA((2,)),
             pltpu.SemaphoreType.DMA((2, 4, 6)),
             pltpu.SemaphoreType.DMA((2, 3)),

time: 122 us -> 116 us (0.951)
  the two profiles are of different devices: /device:TPU:64 before, /device:TPU:1 now
where the time goes in v4:
time: 116 us
  Pallas kernels  113 us (97%)
  local copies, waits for them, and re-layouts  1.57 us (1%)
  between operations  1.29 us (1%)
    pallas_call x1, Pallas kernels, shards(): pl.pallas_call(functools.partial(kernel, (C, G, R, D, K)), name='refine',...  113 us

profile of v4, /device:TPU:1, one launch (start us, length us, event | category | flops | bytes accessed | tf_op | source)
XLA Modules:
  0.0 115.6 jit_solution(13448324342046004701)
XLA Ops:
  1.3 112.7 %refine.1 = (bf16[512,1024]{1,0:T(8,128)(2,1)S(1)}, f32[1,1024]{1,0:T(1,128)S(1)}) custom-call(bf16[512,1024]{1,0:T(8,128)(2,1)} %x_hbm.1, s32[1,512]{1,0:T(1,128)} %bitcast.4, s32[1,512]{1,0:T(1,128)} %bitcast.5, s32[1,512]{1,0:T(1,128)} %seed_hbm.1, f32[1]{0:T(128)S(6)} %copy.11.kappa_hbm), custom_call_target="tpu_custom_call" | custom-call | tf_op jit(solution)/shard_map/refine/pallas_call | solution.py:487
  114.0 1.0 copy.9
  115.0 0.6 copy.10

commit v5 on v4

--- a/solution.py
+++ b/solution.py
@@ -36,6 +36,8 @@
 
 
 def rows_at(index, size):
+    if isinstance(index, int):
+        return pl.ds(index * size, size)
     return pl.ds(pl.multiple_of(index * size, size), size)
 
 
@@ -67,17 +69,6 @@
     z = c // 2
     core = lax.rem(c, 2)
 
-    barrier = pltpu.get_barrier_semaphore()
-    for i in range(1, Z):
-        pl.semaphore_signal(barrier, inc=1, device_id=(lax.rem(z + i, Z) * 2 + core, g), device_id_type=MESH)
-    for i in range(1, G):
-        pl.semaphore_signal(barrier, inc=1, device_id=(c, lax.rem(g + i, G)), device_id_type=MESH)
-
-    @pl.when(core == 0)
-    def _():
-        for i in range(Z):
-            pl.semaphore_signal(barrier, inc=1, device_id=(lax.rem(z + i, Z) * 2 + 1, g), device_id_type=MESH)
-
     chunks = 4
     rstep = R // chunks
     loads = [
@@ -91,6 +82,17 @@
     for load in loads + small:
         load.start()
 
+    barrier = pltpu.get_barrier_semaphore()
+    for i in range(1, Z):
+        pl.semaphore_signal(barrier, inc=1, device_id=(lax.rem(z + i, Z) * 2 + core, g), device_id_type=MESH)
+    for i in range(1, G):
+        pl.semaphore_signal(barrier, inc=1, device_id=(c, lax.rem(g + i, G)), device_id_type=MESH)
+
+    @pl.when(core == 0)
+    def _():
+        for i in range(Z):
+            pl.semaphore_signal(barrier, inc=1, device_id=(lax.rem(z + i, Z) * 2 + 1, g), device_id_type=MESH)
+
     def send(phase, src, dst, device):
         pltpu.make_async_remote_copy(
             src_ref=src, dst_ref=dst, send_sem=send_sem.at[phase], recv_sem=recv_sem.at[phase],
@@ -110,6 +112,8 @@
         def _(j):
             cols = rows_at(j, ncol)
             dst[dst_rows, cols] = nn(lhs, rhs_ref[rhs_rows, cols]).astype(BF16)
+
+    FAR = sorted(range(1, Z), key=lambda i: -min(i, Z - i))
 
     for i in range(chunks):
         loads[i].wait()
@@ -129,26 +133,37 @@
     hot[0:S, 0:R] = onehot(iota((S, R), 0) == jnp.where(moving & (side == 0), lz * G + member, -1))
     product(send_a, slice(None), hot[0:S, 0:R], rows, own)
 
-    pl.semaphore_wait(barrier, Z - 1 + G - 1 + core * Z)
-
-    @pl.when(core == 0)
-    def _():
-        for i in range(1, Z):
-            tz = lax.rem(z + i, Z)
-            send(0, send_a.at[rows_at(tz, G)], mid_a.at[0, rows_at(z, G)], (tz * 2, g))
-        mid_a[0, rows_at(z, G), :] = send_a[rows_at(z, G), :]
-
-    @pl.when(core == 1)
-    def _():
-        for i in range(Z):
-            tz = lax.rem(z + i, Z)
-            pl.semaphore_signal(ready, inc=1, device_id=(tz * 2, g), device_id_type=MESH)
-            send(3, send_a.at[rows_at(tz, G)], mid_a.at[1, rows_at(z, G)], (tz * 2, g))
+    to_cluster = onehot((iota((128, R), 0) == label) & moving)
+    to_member = onehot(iota((128, R), 0) == member)
+    marks = nt(to_cluster, to_member)
+    for i in range(C):
+        mark_s[i] = marks[i:i + 1, :]
+    mark_1[c] = mark_s[c]
 
     def cross_marks():
         for i in range(Z):
             tc = lax.rem(z + i, Z) * 2 + 1 - core
             send(4, mark_s.at[tc], mark_1.at[c], (tc, g))
+
+    pl.semaphore_wait(barrier, Z - 1 + G - 1 + core * Z)
+    for i in range(1, Z):
+        tc = lax.rem(z + i, Z) * 2 + core
+        send(2, mark_s.at[tc], mark_1.at[c], (tc, g))
+    pl.when(core == 1)(cross_marks)
+
+    @pl.when(core == 0)
+    def _():
+        for i in FAR:
+            tz = lax.rem(z + i, Z)
+            send(0, send_a.at[rows_at(tz, G)], mid_a.at[0, rows_at(z, G)], (tz * 2, g))
+        mid_a[0, rows_at(z, G), :] = send_a[rows_at(z, G), :]
+
+    @pl.when(core == 1)
+    def _():
+        for i in FAR + [0]:
+            tz = lax.rem(z + i, Z)
+            pl.semaphore_signal(ready, inc=1, device_id=(tz * 2, g), device_id_type=MESH)
+            send(3, send_a.at[rows_at(tz, G)], mid_a.at[1, rows_at(z, G)], (tz * 2, g))
 
     n = round(G ** 0.5)
     hb = kb // 2
@@ -302,16 +317,6 @@
         hot[0:S, 0:R] = onehot(iota((S, R), 0) == jnp.where(moving & (side == 1), member * Z + lz, -1))
         product(send_b, slice(None), hot[0:S, 0:R], rows, own)
         mid_b[rows_at(g, Z), :] = send_b[rows_at(g, Z), :]
-        to_cluster = onehot((iota((128, R), 0) == label) & moving)
-        to_member = onehot(iota((128, R), 0) == member)
-        marks = nt(to_cluster, to_member)
-        for i in range(C):
-            mark_s[i] = marks[i:i + 1, :]
-        mark_1[c] = mark_s[c]
-        for i in range(1, Z):
-            tc = lax.rem(z + i, Z) * 2 + core
-            send(2, mark_s.at[tc], mark_1.at[c], (tc, g))
-        pl.when(core == 1)(cross_marks)
 
     def other_sends():
         for i in range(1, G):
@@ -332,14 +337,14 @@
 
         @pl.when(core == 1)
         def _():
-            for i in range(1, Z):
+            for i in FAR:
                 tz = lax.rem(z + i, Z)
                 send(5, fwd_b.at[rows_at(tz, G)], landing, (tz * 2 + 1, g))
             landing[...] = fwd_b[rows_at(z, G), :]
 
         @pl.when(core == 0)
         def _():
-            for i in range(Z):
+            for i in FAR + [0]:
                 tz = lax.rem(z + i, Z)
                 send(6, fwd_b.at[rows_at(tz, G)], landing, (tz * 2 + 1, g))
 
@@ -392,7 +397,7 @@
         from_g = (1 - core) * lax.div(q, Z) + core * (q & (G - 1))
         return 2 * from_z + lax.div(index, S), from_g
 
-    kappa = kappa_ref[0]
+    kappa = kappa_ref[0, 0]
     step = S
 
     def expectation(i):
@@ -445,7 +450,8 @@
 
     for it in range(ITERS):
         if it:
-            pl.loop(0, own_steps + 2)(expectation)
+            for i in range(own_steps + 2):
+                expectation(i)
         totals = reduce_scatter(fill_sums)
         squares = [jnp.sum(t * t, axis=-1, keepdims=True) for t in totals]
         length = jnp.maximum(jnp.sqrt(squares[0] + squares[1]), 1.0)
@@ -498,7 +504,7 @@
             pltpu.VMEM((1, R), I32),
             pltpu.VMEM((1, R), I32),
             pltpu.VMEM((1, K), I32),
-            pltpu.SMEM((1,), F32),
+            pltpu.SMEM((1, 1), F32),
             pltpu.VMEM((slots, D), BF16),
             pltpu.VMEM((max(R, K), max(R, K)), BF16),
             pltpu.VMEM((S, D), BF16),
@@ -540,7 +546,7 @@
         new_label.reshape(1, R),
         dest_member.reshape(1, R),
         seed_index,
-        kappa,
+        kappa.reshape(1, 1),
     )
     return centroids, score.reshape(slots)
 

time: 116 us -> 113 us (0.974)
  Pallas kernels: 113 us -> 110 us
    pallas_call x1, Pallas kernels: 113 us -> 110 us  [shards(): pl.pallas_call(functools.partial(kernel, (C, G, R, D, K)), name='refine',...]
where the time goes in v5:
time: 113 us
  Pallas kernels  110 us (97%)
  local copies, waits for them, and re-layouts  1.57 us (1%)
  between operations  1.29 us (1%)
    pallas_call x1, Pallas kernels, shards(): pl.pallas_call(functools.partial(kernel, (C, G, R, D, K)), name='refine',...  110 us

profile of v5, /device:TPU:1, one launch (start us, length us, event | category | flops | bytes accessed | tf_op | source)
XLA Modules:
  0.0 113.1 jit_solution(15807227171841087314)
XLA Ops:
  1.3 110.2 %refine.1 = (bf16[512,1024]{1,0:T(8,128)(2,1)S(1)}, f32[1,1024]{1,0:T(1,128)S(1)}) custom-call(bf16[512,1024]{1,0:T(8,128)(2,1)} %x_hbm.1, s32[1,512]{1,0:T(1,128)} %bitcast.6, s32[1,512]{1,0:T(1,128)} %bitcast.7, s32[1,512]{1,0:T(1,128)} %seed_hbm.1, f32[1,1]{1,0:T(1,128)} %bitcast.4.kappa_hbm), custom_call_target="tpu_custom_call" | custom-call | tf_op jit(solution)/shard_map/refine/pallas_call | solution.py:493
  111.5 1.0 copy.9
  112.5 0.6 copy.10

commit v6 on v5

--- a/solution.py
+++ b/solution.py
@@ -201,14 +201,18 @@
 
     TOP, LOW = pl.ds(0, hb), pl.ds(hb, hb)
 
-    def reduce_scatter(fill, meanwhile=None):
-        for h in range(2):
-            fill(h)
+    def reduce_scatter(fill_far, fill_rest=None, meanwhile=None):
+        for h in range(2):
+            fill_far(h)
             ahead, behind = block(h, 1, 0), block(h, -1, 0)
             for r in ORDER:
                 far = block(h, 2, r)
                 push(0, part.at[h, part_of(far, 0)], relay.at[h, r, TOP], rs_sem.at[h, r, 0], ahead)
                 push(0, part.at[h, part_of(far, 1)], relay.at[h, r, LOW], rs_sem.at[h, r, 1], behind)
+        for h in range(2):
+            if fill_rest is not None:
+                fill_rest(h)
+            ahead, behind = block(h, 1, 0), block(h, -1, 0)
             for r in ORDER:
                 push(0, part.at[h, part_of(block(h, 1, r), 1)], nearer.at[h, r, 0, LOW], rs_sem.at[h, r, 2], ahead)
                 push(0, part.at[h, part_of(block(h, -1, r), 0)], nearer.at[h, r, 1, TOP], rs_sem.at[h, r, 3], behind)
@@ -307,11 +311,13 @@
             cols = pl.ds(pl.multiple_of(h * Dh + j * hcol, hcol), hcol)
             part[h, :, rows_at(j, hcol)] = tn(hot[0:R, 0:K], rows[own, cols]).astype(BF16)
 
-    def fill_sums(h):
-        @pl.loop(0, Dh // hcol)
-        def _(j):
-            cols = pl.ds(pl.multiple_of(h * Dh + j * hcol, hcol), hcol)
-            part[h, :, rows_at(j, hcol)] = nn(weights[...], rows[:, cols]).astype(BF16)
+    def fill_blocks(h, steps):
+        targets = [part_of(block(h, dp, r)) for dp in steps for r in range(n)]
+        lhs = jnp.concatenate([weights[at, :] for at in targets], axis=0)
+        for j in range(Dh // hcol):
+            sums = nn(lhs, rows[:, h * Dh + j * hcol:h * Dh + (j + 1) * hcol]).astype(BF16)
+            for i, at in enumerate(targets):
+                part[h, at, j * hcol:(j + 1) * hcol] = sums[i * kb:(i + 1) * kb, :]
 
     def other_rows():
         hot[0:S, 0:R] = onehot(iota((S, R), 0) == jnp.where(moving & (side == 1), member * Z + lz, -1))
@@ -348,7 +354,7 @@
                 tz = lax.rem(z + i, Z)
                 send(6, fwd_b.at[rows_at(tz, G)], landing, (tz * 2 + 1, g))
 
-    first_blocks = [t.astype(BF16) for t in reduce_scatter(fill_seeds, other_rows)]
+    first_blocks = [t.astype(BF16) for t in reduce_scatter(fill_seeds, None, other_rows)]
     all_gather(first_blocks, other_sends, other_legs)
     sent(0)
     sent(1)
@@ -452,7 +458,7 @@
         if it:
             for i in range(own_steps + 2):
                 expectation(i)
-        totals = reduce_scatter(fill_sums)
+        totals = reduce_scatter(lambda h: fill_blocks(h, (2,)), lambda h: fill_blocks(h, (1, 3, 0)))
         squares = [jnp.sum(t * t, axis=-1, keepdims=True) for t in totals]
         length = jnp.maximum(jnp.sqrt(squares[0] + squares[1]), 1.0)
         all_gather([(t / length).astype(BF16) for t in totals], place_scores if it == ITERS - 1 else None)

time: 113 us -> 111 us (0.982)
  Pallas kernels: 110 us -> 108 us
    pallas_call x1, Pallas kernels: 110 us -> 108 us  [shards(): pl.pallas_call(functools.partial(kernel, (C, G, R, D, K)), name='refine',...]
where the time goes in v6:
time: 111 us
  Pallas kernels  108 us (97%)
  local copies, waits for them, and re-layouts  1.57 us (1%)
  between operations  1.29 us (1%)
    pallas_call x1, Pallas kernels, shards(): pl.pallas_call(functools.partial(kernel, (C, G, R, D, K)), name='refine',...  108 us

profile of v6, /device:TPU:1, one launch (start us, length us, event | category | flops | bytes accessed | tf_op | source)
XLA Modules:
  0.0 111.2 jit_solution(6649437255429410866)
XLA Ops:
  1.3 108.3 %refine.1 = (bf16[512,1024]{1,0:T(8,128)(2,1)S(1)}, f32[1,1024]{1,0:T(1,128)S(1)}) custom-call(bf16[512,1024]{1,0:T(8,128)(2,1)} %x_hbm.1, s32[1,512]{1,0:T(1,128)} %bitcast.6, s32[1,512]{1,0:T(1,128)} %bitcast.7, s32[1,512]{1,0:T(1,128)} %seed_hbm.1, f32[1,1]{1,0:T(1,128)} %bitcast.4.kappa_hbm), custom_call_target="tpu_custom_call" | custom-call | tf_op jit(solution)/shard_map/refine/pallas_call | solution.py:499
  109.6 1.0 copy.9
  110.6 0.6 copy.10

commit v7 on v6

--- a/solution.py
+++ b/solution.py
@@ -207,6 +207,9 @@
             ahead, behind = block(h, 1, 0), block(h, -1, 0)
             for r in ORDER:
                 far = block(h, 2, r)
+                if r == 2:
+                    push(0, part.at[h, part_of(far)], relay.at[h, r], rs_sem.at[h, r, 0], block(h, 2, 0))
+                    continue
                 push(0, part.at[h, part_of(far, 0)], relay.at[h, r, TOP], rs_sem.at[h, r, 0], ahead)
                 push(0, part.at[h, part_of(far, 1)], relay.at[h, r, LOW], rs_sem.at[h, r, 1], behind)
         for h in range(2):
@@ -214,11 +217,16 @@
                 fill_rest(h)
             ahead, behind = block(h, 1, 0), block(h, -1, 0)
             for r in ORDER:
+                if r == 2:
+                    push(0, part.at[h, part_of(block(h, 1, r))], nearer.at[h, r, 0], rs_sem.at[h, r, 2], ahead)
+                    push(0, part.at[h, part_of(block(h, -1, r))], nearer.at[h, r, 1], rs_sem.at[h, r, 3], behind)
+                    continue
                 push(0, part.at[h, part_of(block(h, 1, r), 1)], nearer.at[h, r, 0, LOW], rs_sem.at[h, r, 2], ahead)
                 push(0, part.at[h, part_of(block(h, -1, r), 0)], nearer.at[h, r, 1, TOP], rs_sem.at[h, r, 3], behind)
         if meanwhile is not None:
             meanwhile()
-        for r in ORDER:
+
+        def relayed(r):
             for h in range(2):
                 ahead, behind = block(h, 1, 0), block(h, -1, 0)
                 landed(relay.at[h, r, TOP], rs_sem.at[h, r, 0])
@@ -229,17 +237,32 @@
                 mine = part[h, part_of(block(h, -1, r), 1), :].astype(F32)
                 combined[h, r, LOW, :] = (mine + relay[h, r, LOW, :].astype(F32)).astype(BF16)
                 push(0, combined.at[h, r, LOW], nearer.at[h, r, 1, LOW], rs_sem.at[h, r, 5], behind)
-        for r in ORDER:
+
+        def along_line(r):
             for h in range(2):
-                landed(nearer.at[h, r, 0, LOW], rs_sem.at[h, r, 2])
-                landed(nearer.at[h, r, 1, TOP], rs_sem.at[h, r, 3])
-                landed(nearer.at[h, r, 0, TOP], rs_sem.at[h, r, 4])
-                landed(nearer.at[h, r, 1, LOW], rs_sem.at[h, r, 5])
                 total = part[h, part_of(block(h, 0, r)), :].astype(F32)
+                if r == 2:
+                    landed(nearer.at[h, r, 0], rs_sem.at[h, r, 2])
+                    landed(nearer.at[h, r, 1], rs_sem.at[h, r, 3])
+                    landed(relay.at[h, r], rs_sem.at[h, r, 0])
+                    total = total + relay[h, r].astype(F32)
+                else:
+                    landed(nearer.at[h, r, 0, LOW], rs_sem.at[h, r, 2])
+                    landed(nearer.at[h, r, 1, TOP], rs_sem.at[h, r, 3])
+                    landed(nearer.at[h, r, 0, TOP], rs_sem.at[h, r, 4])
+                    landed(nearer.at[h, r, 1, LOW], rs_sem.at[h, r, 5])
                 total = total + nearer[h, r, 0].astype(F32) + nearer[h, r, 1].astype(F32)
                 line[h, r] = total.astype(BF16)
                 if r:
                     push(0, line.at[h, r], line_in.at[h, r - 1], rs_line_sem.at[h, r - 1], block(h, 0, r))
+
+        relayed(1)
+        relayed(3)
+        along_line(2)
+        relayed(0)
+        along_line(1)
+        along_line(3)
+        along_line(0)
         totals = []
         for h in range(2):
             total = line[h, 0].astype(F32)

time: 111 us -> 110 us (level)
    pallas_call x1, Pallas kernels: 108 us -> 107 us  [shards(): pl.pallas_call(functools.partial(kernel, (C, G, R, D, K)), name='refine',...]
where the time goes in v7:
time: 110 us
  Pallas kernels  107 us (97%)
  local copies, waits for them, and re-layouts  1.57 us (1%)
  between operations  1.29 us (1%)
    pallas_call x1, Pallas kernels, shards(): pl.pallas_call(functools.partial(kernel, (C, G, R, D, K)), name='refine',...  107 us

profile of v7, /device:TPU:1, one launch (start us, length us, event | category | flops | bytes accessed | tf_op | source)
XLA Modules:
  0.0 109.8 jit_solution(16803619940460734366)
XLA Ops:
  1.3 107.0 %refine.1 = (bf16[512,1024]{1,0:T(8,128)(2,1)S(1)}, f32[1,1024]{1,0:T(1,128)S(1)}) custom-call(bf16[512,1024]{1,0:T(8,128)(2,1)} %x_hbm.1, s32[1,512]{1,0:T(1,128)} %bitcast.6, s32[1,512]{1,0:T(1,128)} %bitcast.7, s32[1,512]{1,0:T(1,128)} %seed_hbm.1, f32[1,1]{1,0:T(1,128)} %bitcast.4.kappa_hbm), custom_call_target="tpu_custom_call" | custom-call | tf_op jit(solution)/shard_map/refine/pallas_call | solution.py:522
  108.3 1.0 copy.9
  109.2 0.6 copy.10
